TPU v7x, 256 devices: a whole 4x4x8 slice. The times are simulated.
256 devices in a mesh: gx: 16 (over y_lo, z), gy: 4 (over x), gz: 4 (over y_hi, core).
Axes of the slice: x: 4, y: 4 (y_hi: 2, y_lo: 2; y = y_hi * 2 + y_lo), z: 8, core: 2. Of those that a mesh axis runs over, the one named last changes fastest.
Arguments:
- positions: float32 [16, 4, 4, 3, 2048], P('gx', 'gy', 'gz'), may hold values from 0 to 1
- charges: float32 [16, 4, 4, 2048], P('gx', 'gy', 'gz'), may hold values from -1.8 to 1.8
- masses: float32 [16, 4, 4, 2048], P('gx', 'gy', 'gz'), may hold values from 1 to 16
- weights: float32 [16, 4, 4, 512], P('gx', 'gy', 'gz'), may hold values from 0 to 1, as said below
- mapping: int32 [16, 4, 4, 2048], P('gx', 'gy', 'gz'), may hold values from 0 to 511, as said below
- atom_lists: int32 [16, 4, 4, 16, 27], P('gx', 'gy', 'gz'), may hold values from 0 to 431, as said below
- bead_lists: int32 [16, 4, 4, 4, 12], P('gx', 'gy', 'gz'), may hold values from 0 to 107, as said below
- leaving: int32 [16, 4, 4, 2, 128], P('gx', 'gy', 'gz'), may hold values from 0 to 511, as said below
Outputs:
- forces: float32 [16, 4, 4, 3, 2048], P('gx', 'gy', 'gz')
- arrivals: float32 [16, 4, 4, 2, 8, 128], P('gx', 'gy', 'gz')
Inputs may be any that keep to these rules, and one draw needn't show every extreme that they name: `mapping`: every bead number of a cell names exactly 4 atoms of that cell. `atom_lists`: entry c of every row names a tile of neighbourhood cell c, and within one cell and one column the 16 rows name 16 different tiles. `bead_lists`: the entries of one row are distinct. `leaving`: the 256 entries of a cell are distinct. With s = (i + 0.5) / 16 for a cell at slab index i: all weights are 1 where |s - 0.5| < 0.15 and all are 0 where |s - 0.5| >= 0.35.
All inputs are finite; a program needn't handle non-finite values.
Results may differ from a plain program's by a relative error of at most 0.0003.
Values sent between devices are 32-bit elements; how exact they have to be, the bound alone decides.
A program may use at most 64 MiB of HBM per device.

v0:
```python
import jax
import jax.numpy as jnp
from jax import lax
from jax.sharding import PartitionSpec as P

soft_core = 0.01
eps_coarse = 2.0
sigma_sq = 0.25
exact = lax.Precision.HIGHEST


def padded(x, sides, width):
    for axis, dim in sides:
        size, length = (lax.axis_size(axis), x.shape[dim])
        up = [(i, (i + 1) % size) for i in range(size)]
        down = [(j, i) for i, j in up]
        last = lax.slice_in_dim(x, length - width, length, axis=dim)
        first = lax.slice_in_dim(x, 0, width, axis=dim)
        before = lax.ppermute(last, axis, up)
        after = lax.ppermute(first, axis, down)
        x = jnp.concatenate([before, x, after], axis=dim)
    return x


def from_behind(x, axis, by):
    size = lax.axis_size(axis)
    return lax.ppermute(x, axis, [(i, (i + by) % size) for i in range(size)])


def neighbour_offsets():
    unit_steps = jnp.arange(3, dtype=jnp.float32) - 1.0
    shift_x = jnp.broadcast_to(unit_steps[:, None, None], (3, 3, 3))
    shift_y = jnp.broadcast_to(unit_steps[None, :, None], (3, 3, 3))
    shift_z = jnp.broadcast_to(unit_steps[None, None, :], (3, 3, 3))
    return jnp.stack([shift_x, shift_y, shift_z], axis=3).reshape(27, 3, 1)


def atom_tile(own_rows, listed):
    other = jnp.moveaxis(listed, 1, 0)
    displace = own_rows[:3, :, None, None] - other[:3, None, :, :]
    dist_sq = jnp.sum(displace * displace, axis=0)
    inv_root = lax.rsqrt(dist_sq + soft_core)
    strength = (
        (own_rows[3] * own_rows[4])[:, None, None]
        * (other[3] * other[4])[None, :, :]
        * (inv_root * inv_root * inv_root)
    )
    return jnp.sum(strength[None] * displace, axis=(2, 3))


def coarse_tile(own_rows, listed):
    other = jnp.moveaxis(listed, 1, 0)
    displace = own_rows[:3, :, None, None] - other[:3, None, :, :]
    dist_sq = jnp.sum(displace * displace, axis=0)
    strength = (
        eps_coarse
        * jnp.exp(-dist_sq / sigma_sq)
        * (1.0 - own_rows[3][:, None, None] * other[3][None, :, :])
    )
    return jnp.sum(strength[None] * displace, axis=(2, 3))


def bead_table(label, bead_count):
    return (label[None, :] == jnp.arange(bead_count, dtype=jnp.int32)[:, None]).astype(jnp.float32)


def listed_forces(near_rows, own_rows, lists, tile_fn):
    width = own_rows.shape[0]
    tile_count = own_rows.shape[1] // 128
    near_flat = jnp.moveaxis(near_rows.reshape(27, width, tile_count, 128), 2, 1).reshape(
        27 * tile_count, width * 128
    )
    own_tiles = jnp.moveaxis(own_rows.reshape(width, tile_count, 128), 1, 0)
    tile_ids = jnp.arange(27 * tile_count, dtype=jnp.int32)

    def one_tile(member):
        own_block, listed = member
        selector = (listed[:, None] == tile_ids[None, :]).astype(jnp.float32)
        picked = jnp.dot(selector, near_flat, precision=exact, preferred_element_type=jnp.float32)
        return tile_fn(own_block, picked.reshape(listed.shape[0], width, 128))

    result = lax.map(one_tile, (own_tiles, lists))
    return jnp.moveaxis(result, 0, 1).reshape(3, -1)


def per_device(positions, charges, masses, weights, mapping, atom_lists, bead_lists, leaving):
    own_pos = positions[0, 0, 0]
    own_charge = charges[0, 0, 0]
    own_mass = masses[0, 0, 0]
    own_weight = weights[0, 0, 0]
    own_label = mapping[0, 0, 0]
    atom_count = own_pos.shape[1]
    bead_count = own_weight.shape[0]
    table = bead_table(own_label, bead_count)
    atom_weight = jnp.dot(own_weight, table, precision=exact, preferred_element_type=jnp.float32)
    mass_sum = jnp.dot(table, own_mass, precision=exact, preferred_element_type=jnp.float32)
    centres = (
        jnp.dot(
            own_mass[None] * own_pos, table.T, precision=exact, preferred_element_type=jnp.float32
        )
        / mass_sum
    )
    offsets = neighbour_offsets()
    own_atoms = jnp.concatenate([own_pos, own_charge[None], atom_weight[None]], axis=0)
    own_beads = jnp.concatenate([centres, own_weight[None]], axis=0)
    record_rows = jnp.concatenate(
        [own_atoms, own_mass[None], own_label.astype(jnp.float32)[None]], axis=0
    )
    near_rows = padded(record_rows[None, None, None], (("gx", 0), ("gy", 1), ("gz", 2)), 1)
    flattened = near_rows.reshape(27, 7, atom_count)

    def rebuild(record):
        cell_table = bead_table(record[6].astype(jnp.int32), bead_count)
        cell_mass = jnp.dot(
            cell_table, record[5], precision=exact, preferred_element_type=jnp.float32
        )
        centre_pos = (
            jnp.dot(
                record[5][None] * record[:3],
                cell_table.T,
                precision=exact,
                preferred_element_type=jnp.float32,
            )
            / cell_mass
        )
        weight_max = jnp.max(jnp.where(cell_table > 0.5, record[4][None, :], -1.0), axis=1)
        return jnp.concatenate([centre_pos, weight_max[None]], axis=0)

    near_beads = lax.map(rebuild, flattened)
    near_atoms = flattened[:, :5]
    near_atoms = near_atoms.at[:, :3].add(offsets)
    near_beads = near_beads.at[:, :3].add(offsets)
    atomic_force = listed_forces(near_atoms, own_atoms, atom_lists[0, 0, 0], atom_tile)
    coarse_force = listed_forces(near_beads, own_beads, bead_lists[0, 0, 0], coarse_tile)
    scaled_coarse = coarse_force / mass_sum[None]
    forces = atomic_force + own_mass[None] * jnp.dot(
        scaled_coarse, table, precision=exact, preferred_element_type=jnp.float32
    )
    molecule_force = jnp.dot(forces, table.T, precision=exact, preferred_element_type=jnp.float32)
    payload = jnp.concatenate([centres, molecule_force, own_weight[None], mass_sum[None]], axis=0)
    leave_lists = leaving[0, 0, 0]
    bead_ids = jnp.arange(bead_count, dtype=jnp.int32)[:, None]
    pick_up = (leave_lists[0][None, :] == bead_ids).astype(jnp.float32)
    pick_down = (leave_lists[1][None, :] == bead_ids).astype(jnp.float32)
    upward = jnp.dot(payload, pick_up, precision=exact, preferred_element_type=jnp.float32)
    downward = jnp.dot(payload, pick_down, precision=exact, preferred_element_type=jnp.float32)
    from_lower = from_behind(upward, "gx", 1)
    from_higher = from_behind(downward, "gx", -1)
    from_lower = from_lower.at[0].add(-1.0)
    from_higher = from_higher.at[0].add(1.0)
    arrivals = jnp.stack([from_lower, from_higher], axis=0)
    return (forces[None, None, None], arrivals[None, None, None])


def solution(mesh):
    placed = (
        P("gx", "gy", "gz", None, None),
        P("gx", "gy", "gz", None),
        P("gx", "gy", "gz", None),
        P("gx", "gy", "gz", None),
        P("gx", "gy", "gz", None),
        P("gx", "gy", "gz", None, None),
        P("gx", "gy", "gz", None, None),
        P("gx", "gy", "gz", None, None),
    )
    return jax.shard_map(
        per_device,
        mesh=mesh,
        in_specs=placed,
        out_specs=(P("gx", "gy", "gz", None, None), P("gx", "gy", "gz", None, None, None)),
        check_vma=False,
    )
```

profile of v0, /device:TPU:30, one launch (start us, length us, event | category | flops | bytes accessed | tf_op | source)
XLA Modules:
  0.0 240.5 jit_solution(5891872856664729613)
XLA Ops:
  2.2 2.1 fusion.34
  5.0 2.0 collective-permute-start
  7.0 4.2 %collective-permute-start.1 = (f32[1,1,1,7,2048]{4,3,2,1,0:T(8,128)S(1)}, f32[1,1,1,7,2048]{4,3,2,1,0:T(8,128)S(1)}, u32[]{:S(2)}, u32[]{:S(2)}) collective-permute-start(f32[1,1,1,7,2048]{4,3,2,1,0:T(8,128)S(1)} %bitcast.198), channel_id=1, source_target_pairs={{16,0},{32,16},{48,32},{64,48},{80,64},{96,80},{112,96},{128,112},... | collective-permute-start | bytes 172040 | tf_op jit(solution)/shard_map/ppermute | solution.py:20
  11.2 2.6 %fusion.32 = f32[1,512]{1,0:T(1,128)S(1)} fusion(s32[2048]{0:T(1024)} %bitcast.223, f32[1,1,1,2048]{3,2,1,0:T(1,128)} %param.24), kind=kOutput, calls=%fused_computation.60 | convolution fusion | flops 13631488 | bytes 18432 | tf_op jit(solution)/shard_map/dot_general | solution.py:96
  18.0 2.4 collective-permute-done.2
  22.5 3.2 %collective-permute-start.5 = (f32[3,3,1,7,2048]{4,2,3,1,0:T(1,128)S(1)}, f32[3,3,1,7,2048]{4,2,3,1,0:T(1,128)S(1)}, u32[]{:S(2)}, u32[]{:S(2)}) collective-permute-start(f32[3,3,1,7,2048]{4,2,3,1,0:T(1,128)S(1)} %copy.44), channel_id=1, source_target_pairs={{1,0},{2,1},{3,2},{0,3},{5,4},{6,5},{7,6},{4,7},{9,8},{10,9},{11,1... | collective-permute-start | bytes 1548296 | tf_op jit(solution)/shard_map/ppermute | solution.py:20
  26.1 10.7 %collective-permute-done.4 = f32[3,3,1,7,2048]{4,2,3,1,0:T(1,128)S(1)} collective-permute-done((f32[3,3,1,7,2048]{4,2,3,1,0:T(1,128)S(1)}, f32[3,3,1,7,2048]{4,2,3,1,0:T(1,128)S(1)}, u32[]{:S(2)}, u32[]{:S(2)}) %collective-permute-start.4) | collective-permute-done | bytes 516128 | tf_op jit(solution)/shard_map/ppermute | solution.py:19
  37.4 128.2 %while.36 = (s32[]{:T(128)}, f32[27,4,512]{2,1,0:T(4,128)S(1)}, f32[27,7,2048]{2,1,0:T(8,128)S(1)}, s32[]{:T(128)}, s32[]{:T(128)}, /*index=5*/s32[]{}, s32[]{}, s32[]{}) while((s32[]{:T(128)}, f32[27,4,512]{2,1,0:T(4,128)S(1)}, f32[27,7,2048]{2,1,0:T(8,128)S(1)}, s32[]{:T(128)}, s32[]{:T(128)}, /*index=5*/s32[]{}, s32[]{}, s32[]{}) %tuple.92), condition=%wide.region_6.7_spmd, body=%wide.region_4.6_spmd.sunk | while | flops 57682948 | bytes 161937 | solution.py:129
  37.6 1.9 fusion.78
  39.6 2.0 fusion.79
  44.3 2.0 fusion.79
  47.1 1.9 fusion.78
  49.0 2.0 fusion.79
  51.9 1.9 fusion.78
  53.8 2.0 fusion.79
  58.5 2.0 fusion.79
  61.3 1.9 fusion.78
  63.3 2.0 fusion.79
  66.1 1.9 fusion.78
  68.0 2.0 fusion.79
  72.7 2.0 fusion.79
  75.6 1.9 fusion.78
  77.5 2.0 fusion.79
  80.3 1.9 fusion.78
  82.2 2.0 fusion.79
  87.0 2.0 fusion.79
  91.7 2.0 fusion.79
  96.4 2.0 fusion.79
  101.2 2.0 fusion.79
  105.9 2.0 fusion.79
  110.7 2.0 fusion.79
  115.4 2.0 fusion.79
  120.2 2.0 fusion.79
  124.9 2.0 fusion.79
  129.6 2.0 fusion.79
  134.4 2.0 fusion.79
  139.1 2.0 fusion.79
  143.9 2.0 fusion.79
  148.6 2.0 fusion.79
  153.3 2.0 fusion.79
  158.1 2.0 fusion.79
  162.8 2.0 fusion.79
  165.9 2.0 scatter-add.15
  168.0 7.8 %while.38 = (s32[]{:T(128)}, f32[4,3,128]{2,1,0:T(4,128)S(1)}, f32[4,4,128]{2,1,0:T(4,128)S(1)}, s32[4,12]{1,0:T(4,128)}, f32[108,512]{1,0:T(8,128)S(1)}, /*index=5*/s32[]{:T(128)}) while((s32[]{:T(128)}, f32[4,3,128]{2,1,0:T(4,128)S(1)}, f32[4,4,128]{2,1,0:T(4,128)S(1)}, s32[4,12]{1,0:T(4,128)}, f32[108,512]{1,0:T(8,128)S(1)}, ...), condition=%wide.region_10.11_spmd.clone, body=%wide.region_7.10_spmd.clone.sunk | while | flops 12485522 | bytes 3562721 | solution.py:82
  175.8 2.7 %scatter-add.14 = f32[27,5,2048]{2,1,0:T(8,128)S(1)} dynamic-update-slice(f32[27,5,2048]{2,1,0:T(8,128)S(1)} %bitcast.188, f32[27,3,2048]{2,1,0:T(4,128)S(1)} %slice_add_fusion, s32[]{:T(128)} %constant.155.clone.1, s32[]{:T(128)} %constant.155.clone.1, s32[]{:T(128)} %constant.155.clone.1) | dynamic-update-slice | bytes 1327108 | tf_op jit(solution)/shard_map/scatter-add | solution.py:131
  179.7 50.8 %while.37 = (s32[]{:T(128)}, f32[16,3,128]{2,1,0:T(4,128)S(1)}, f32[16,5,128]{2,0,1:T(8,128)S(1)}, s32[16,27]{1,0:T(8,128)}, f32[432,640]{1,0:T(8,128)S(1)}, /*index=5*/s32[]{:T(128)}, s32[]{:T(128)}, s32[]{}, s32[]{}) while((s32[]{:T(128)}, f32[16,3,128]{2,1,0:T(4,128)S(1)}, f32[16,5,128]{2,0,1:T(8,128)S(1)}, s32[16,27]{1,0:T(8,128)}, ...), condition=%wide.region_3.4_spmd.clone, body=%wide.region_0.3_spmd.clone.sunk | while | flops 99326480 | bytes 8740305 | solution.py:82
  231.9 1.9 fusion.30
  234.3 4.2 %collective-permute-start.7 = (f32[8,128]{1,0:T(8,128)S(1)}, f32[8,128]{1,0:T(8,128)S(1)}, u32[]{:S(2)}, u32[]{:S(2)}) collective-permute-start(f32[8,128]{1,0:T(8,128)S(1)} %fusion.44), channel_id=1, source_target_pairs={{0,240},{16,0},{32,16},{48,32},{64,48},{80,64},{96,80},{112,96},{1... | collective-permute-start | bytes 12296 | tf_op jit(solution)/shard_map/ppermute | solution.py:27
  (438 shorter events, 132.5 us)
Async XLA Ops:
  0.6 15.4 %copy-start = (f32[1,1,1,3,2048]{4,2,3,1,0:T(1,128)S(1)}, f32[1,1,1,3,2048]{4,2,3,1,0:T(1,128)}, u32[]{:S(2)}) copy-start(f32[1,1,1,3,2048]{4,2,3,1,0:T(1,128)} %param.22) | copy-start | bytes 73732
  0.6 15.4 %copy-start.3 = (s32[1,1,1,2048]{3,2,1,0:T(1,128)S(1)}, s32[1,1,1,2048]{3,2,1,0:T(1,128)}, u32[]{:S(2)}) copy-start(s32[1,1,1,2048]{3,2,1,0:T(1,128)} %param.26) | copy-start | bytes 24580
  0.7 15.4 %copy-start.2 = (f32[1,1,1,2048]{3,2,1,0:T(1,128)S(1)}, f32[1,1,1,2048]{3,2,1,0:T(1,128)}, u32[]{:S(2)}) copy-start(f32[1,1,1,2048]{3,2,1,0:T(1,128)} %param.24) | copy-start | bytes 24580
  5.0 8.9 %collective-permute-start = (f32[1,1,1,7,2048]{4,3,2,1,0:T(8,128)S(1)}, f32[1,1,1,7,2048]{4,3,2,1,0:T(8,128)S(1)}, u32[]{:S(2)}, u32[]{:S(2)}) collective-permute-start(f32[1,1,1,7,2048]{4,3,2,1,0:T(8,128)S(1)} %bitcast.197), channel_id=1, source_target_pairs={{0,16},{16,32},{32,48},{48,64},{64,80},{80,96},{96,112},{112,128},... | collective-permute-start | bytes 172040 | tf_op jit(solution)/shard_map/ppermute | solution.py:19
  7.0 6.9 %collective-permute-start.1 = (f32[1,1,1,7,2048]{4,3,2,1,0:T(8,128)S(1)}, f32[1,1,1,7,2048]{4,3,2,1,0:T(8,128)S(1)}, u32[]{:S(2)}, u32[]{:S(2)}) collective-permute-start(f32[1,1,1,7,2048]{4,3,2,1,0:T(8,128)S(1)} %bitcast.198), channel_id=1, source_target_pairs={{16,0},{32,16},{48,32},{64,48},{80,64},{96,80},{112,96},{128,112},... | collective-permute-start | bytes 172040 | tf_op jit(solution)/shard_map/ppermute | solution.py:20
  14.0 12.1 %copy-start.4 = (f32[1,1,1,512]{3,2,1,0:T(1,128)S(1)}, f32[1,1,1,512]{3,2,1,0:T(1,128)}, u32[]{:S(2)}) copy-start(f32[1,1,1,512]{3,2,1,0:T(1,128)} %param.25) | copy-start | bytes 6148
  14.0 6.4 %collective-permute-start.2 = (f32[3,1,1,7,2048]{4,3,2,1,0:T(8,128)S(1)}, f32[3,1,1,7,2048]{4,3,2,1,0:T(8,128)S(1)}, u32[]{:S(2)}, u32[]{:S(2)}) collective-permute-start(f32[3,1,1,7,2048]{4,3,2,1,0:T(8,128)S(1)} %pad_maximum_fusion.2), channel_id=1, source_target_pairs={{0,4},{4,8},{8,12},{12,0},{1,5},{5,9},{9,13},{13,1},{2,6},{6,10},{... | collective-permute-start | bytes 516104 | tf_op jit(solution)/shard_map/ppermute | solution.py:19
  14.5 7.3 %collective-permute-start.3 = (f32[3,1,1,7,2048]{4,3,2,1,0:T(8,128)S(1)}, f32[3,1,1,7,2048]{4,3,2,1,0:T(8,128)S(1)}, u32[]{:S(2)}, u32[]{:S(2)}) collective-permute-start(f32[3,1,1,7,2048]{4,3,2,1,0:T(8,128)S(1)} %pad_maximum_fusion.2), channel_id=1, source_target_pairs={{4,0},{8,4},{12,8},{0,12},{5,1},{9,5},{13,9},{1,13},{6,2},{10,6},{... | collective-permute-start | bytes 516104 | tf_op jit(solution)/shard_map/ppermute | solution.py:20
  16.1 10.0 %copy-start.1 = (f32[1,1,1,2048]{3,2,1,0:T(1,128)S(1)}, f32[1,1,1,2048]{3,2,1,0:T(1,128)}, u32[]{:S(2)}) copy-start(f32[1,1,1,2048]{3,2,1,0:T(1,128)} %param.23) | copy-start | bytes 24580
  16.1 10.0 %copy-start.5 = (s32[1,1,1,2,128]{4,3,2,1,0:T(2,128)S(1)}, s32[1,1,1,2,128]{4,3,2,1,0:T(2,128)}, u32[]{:S(2)}) copy-start(s32[1,1,1,2,128]{4,3,2,1,0:T(2,128)} %param.29) | copy-start | bytes 3076
  22.4 14.4 %collective-permute-start.4 = (f32[3,3,1,7,2048]{4,2,3,1,0:T(1,128)S(1)}, f32[3,3,1,7,2048]{4,2,3,1,0:T(1,128)S(1)}, u32[]{:S(2)}, u32[]{:S(2)}) collective-permute-start(f32[3,3,1,7,2048]{4,2,3,1,0:T(1,128)S(1)} %copy.44), channel_id=1, source_target_pairs={{0,1},{1,2},{2,3},{3,0},{4,5},{5,6},{6,7},{7,4},{8,9},{9,10},{10,1... | collective-permute-start | bytes 1548296 | tf_op jit(solution)/shard_map/ppermute | solution.py:19
  22.5 14.5 %collective-permute-start.5 = (f32[3,3,1,7,2048]{4,2,3,1,0:T(1,128)S(1)}, f32[3,3,1,7,2048]{4,2,3,1,0:T(1,128)S(1)}, u32[]{:S(2)}, u32[]{:S(2)}) collective-permute-start(f32[3,3,1,7,2048]{4,2,3,1,0:T(1,128)S(1)} %copy.44), channel_id=1, source_target_pairs={{1,0},{2,1},{3,2},{0,3},{5,4},{6,5},{7,6},{4,7},{9,8},{10,9},{11,1... | collective-permute-start | bytes 1548296 | tf_op jit(solution)/shard_map/ppermute | solution.py:20
  234.0 5.8 %collective-permute-start.6 = (f32[8,128]{1,0:T(8,128)S(1)}, f32[8,128]{1,0:T(8,128)S(1)}, u32[]{:S(2)}, u32[]{:S(2)}) collective-permute-start(f32[8,128]{1,0:T(8,128)S(1)} %fusion.43), channel_id=1, source_target_pairs={{0,16},{16,32},{32,48},{48,64},{64,80},{80,96},{96,112},{112,128},... | collective-permute-start | bytes 12296 | tf_op jit(solution)/shard_map/ppermute | solution.py:27
  234.3 5.5 %collective-permute-start.7 = (f32[8,128]{1,0:T(8,128)S(1)}, f32[8,128]{1,0:T(8,128)S(1)}, u32[]{:S(2)}, u32[]{:S(2)}) collective-permute-start(f32[8,128]{1,0:T(8,128)S(1)} %fusion.44), channel_id=1, source_target_pairs={{0,240},{16,0},{32,16},{48,32},{64,48},{80,64},{96,80},{112,96},{1... | collective-permute-start | bytes 12296 | tf_op jit(solution)/shard_map/ppermute | solution.py:27
where the time goes:
time: 243 us; the launch traced here: 241 us
  matrix products  124 us (51%)
  other arithmetic  56.7 us (23%)
  local copies, waits for them, and re-layouts  24.7 us (10%)
  starting transfers between devices  15.9 us (7%)
  waiting for transfers between devices  15.1 us (6%)
  loops' own time  2.76 us (1%)
    dot_general x27, matrix products, rebuild(): jnp.dot(record[5][None] * record[:3], cell_table.T, precision=exact, pref...  52.7 us
    dot_general x27, matrix products, rebuild(): jnp.dot(cell_table, record[5], precision=exact, preferred_element_type=jn...  52.1 us
    reduce_max x27, other arithmetic, rebuild(): jnp.max(jnp.where(cell_table > 0.5, record[4][None, :], -1.0), axis=1)  21 us
    eq x20, local copies, waits for them, and re-layouts, one_tile(): selector = (listed[:, None] == tile_ids[None, :]).astype(jnp.float32)  13.9 us
    ppermute x3, waiting for transfers between devices, padded(): before = lax.ppermute(last, axis, up)  13 us
    reduce_sum x16, other arithmetic, atom_tile(): return jnp.sum(strength[None] * displace, axis=(2, 3))  11 us
    reduce_sum x16, other arithmetic, atom_tile(): dist_sq = jnp.sum(displace * displace, axis=0)  10.7 us
    dot_general x20, matrix products, one_tile(): jnp.dot(selector, near_flat, precision=exact, preferred_element_type=jnp....  9.2 us
  transfers between devices with their start and end apart: 8, of which 4 were waited for; matrix products, arithmetic and copies ran while one was open for 2% of the time, Pallas kernels for 0%

commit v1 on v0

v1 whole, which is shorter than its diff:
```python
import functools

import jax
import jax.numpy as jnp
from jax import lax
from jax.experimental import pallas as pl
from jax.experimental.pallas import tpu as pltpu
from jax.sharding import PartitionSpec as P

soft_core = 0.01
inv_sigma_sq = 4.0
f32, bf16, i32 = jnp.float32, jnp.bfloat16, jnp.int32
MESH = pl.DeviceIdType.MESH
TILES = 20


def slot_of(a, b, c):
    return 9 * (a + 1) + 3 * (b + 1) + (c + 1)


OWN = slot_of(0, 0, 0)
ROUTE = {}
for _s in (-1, 1):
    ROUTE[slot_of(0, 0, _s)] = (OWN, "gz", -_s)
    for _c in (-1, 0, 1):
        ROUTE[slot_of(_s, 0, _c)] = (slot_of(0, 0, _c), "gx", -_s)
        ROUTE[slot_of(0, _s, _c)] = (slot_of(0, 0, _c), "gy", -_s)
        ROUTE[slot_of(_s, _s, _c)] = (slot_of(0, _s, _c), "gx", -_s)
        ROUTE[slot_of(-_s, _s, _c)] = (slot_of(-_s, 0, _c), "gy", -_s)

WAVES = (
    [slot_of(0, 0, c) for c in (-1, 1)]
    + [slot_of(s, 0, 0) for s in (-1, 1)]
    + [slot_of(0, s, 0) for s in (-1, 1)],
    [slot_of(s, t, 0) for s in (-1, 1) for t in (-1, 1)]
    + [slot_of(s, 0, c) for c in (-1, 1) for s in (-1, 1)]
    + [slot_of(0, s, c) for c in (-1, 1) for s in (-1, 1)],
    [slot_of(s, t, c) for c in (-1, 1) for s in (-1, 1) for t in (-1, 1)],
)


def split3(v):
    h = v.astype(bf16).astype(f32)
    r = v - h
    m = r.astype(bf16).astype(f32)
    return h, m, r - m


def dot_nt(a, b):
    return lax.dot_general(a, b, (((1,), (1,)), ((), ())), preferred_element_type=f32)


def dot_nn(a, b):
    return jnp.dot(a, b, preferred_element_type=f32)


def stack3(scr, rows, value):
    h, m, l = split3(value)
    scr[0:rows, :] = h
    scr[rows : 2 * rows, :] = m
    scr[2 * rows : 3 * rows, :] = l


def place():
    sub = lax.broadcasted_iota(i32, (10, 8, 128), 1)
    return sub & 3, sub < 4


def up_rows(x, by):
    return pltpu.roll(x, by % 8, 1)


def fourth_to_all(v, row):
    u = jnp.where(row == 3, v, 0.0)
    u = u + up_rows(u, -1)
    return u + up_rows(u, -2)


def squares_to_fourth(v):
    sq = v * v
    return up_rows(sq, 1) + up_rows(sq, 2) + up_rows(sq, 3)


def interleave(groups, low):
    even, odd = [], []
    for g, k in zip(groups[0::2], groups[1::2], strict=True):
        even.append(jnp.where(low, g, up_rows(k, 4)))
        odd.append(jnp.where(low, up_rows(g, 4), k))
    zero = jnp.zeros((10, 8, 128), f32)
    return (
        jnp.concatenate(even + [zero], axis=1),
        jnp.concatenate(odd + [zero], axis=1),
    )


def build_cell(slot, pay, bmat, rmat):
    row, low = place()
    v = pay[slot].reshape(10, 8, 128)
    offset = (slot // 9 - 1, slot // 3 % 3 - 1, slot % 3 - 1)
    for axis in range(3):
        if offset[axis]:
            v = v + jnp.where(row == axis, float(offset[axis]), 0.0)
    atoms, beads = v[:8], v[8:]
    scaled = jnp.where(row[:8] == 3, atoms, atoms * fourth_to_all(atoms, row[:8]))
    rmat[pl.ds(slot * TILES * 4, 64), :] = scaled.reshape(64, 128)
    rmat[pl.ds(slot * TILES * 4 + 64, 16), :] = beads.reshape(16, 128)
    h, m, l = split3(jnp.where(row == 3, squares_to_fourth(v), v))
    h1 = jnp.where(row == 3, 1.0, h)
    m1 = jnp.where(row == 3, 1.0, m)
    even, odd = interleave((h, h1, m, m1, l, h1), low)
    bmat[pl.ds(slot * 10, 10), 0] = even.astype(bf16)
    bmat[pl.ds(slot * 10, 10), 1] = odd.astype(bf16)


def build_own(pay, amat, wcol):
    row, low = place()
    v = pay[OWN].reshape(10, 8, 128)
    atom = lax.broadcasted_iota(i32, (10, 8, 128), 0) < 8
    near = squares_to_fourth(v) + jnp.where(atom, soft_core, 0.0)
    h, m, l = split3(jnp.where(row == 3, near, v))
    a0 = jnp.where(row == 3, 1.0, -2.0 * h)
    a1 = jnp.where(row == 3, h, -2.0 * m)
    a3 = jnp.where(row == 3, m, -2.0 * m)
    a5 = jnp.where(row == 3, l, -2.0 * l)
    even, odd = interleave((a0, a1, a0, a3, a0, a5), low)
    for t in range(TILES):
        half = (even, odd)[t % 2][t // 2]
        amat[t * 128 : t * 128 + 128, :] = half.T.astype(bf16)
    for b in range(4):
        r = 64 + 4 * b + 3
        wide = jnp.broadcast_to(pay[OWN, r : r + 1, :], (128, 128))
        wcol[b * 128 : b * 128 + 128, :] = wide.T


def distances(t, cells, lists, amat, bmat, dist):
    a = amat[pl.ds(pl.multiple_of(t * 128, 128), 128), :]
    for at in range(0, len(cells), 2):
        some = cells[at : at + 2]
        tiles = []
        for c in some:
            e = lists[0, 0, 0, t, c] + 4 * c
            tiles.append(bmat[e // 2, e % 2])
        b = tiles[0] if len(some) == 1 else jnp.concatenate(tiles, axis=1)
        dist[:, at * 128 : (at + len(some)) * 128] = dot_nn(a, b)


def add_columns(gather, first_row, rows, lane0, sums):
    lane = lax.broadcasted_iota(i32, (rows, 128), 1)
    got = gather[pl.ds(first_row, rows), :]
    for k in range(4):
        got = jnp.where(lane == lane0 + k, jnp.sum(sums[k], axis=1, keepdims=True), got)
    gather[pl.ds(first_row, rows), :] = got


def accumulate(t, cells, first, last, lists, rmat, dist, total, gather):
    rows = 32
    for g in range(128 // rows):
        at = pl.multiple_of(t * 128 + g * rows, rows)
        if first:
            acc = [jnp.zeros((rows, 128), f32) for _ in range(4)]
        else:
            acc = [total[k, pl.ds(at, rows), :] for k in range(4)]
        for n, c in enumerate(cells):
            e = 4 * (lists[0, 0, 0, t, c] + 4 * c)
            s = lax.rsqrt(dist[g * rows : (g + 1) * rows, n * 128 : n * 128 + 128])
            s = s * s * s
            for k in range(4):
                line = rmat[pl.ds(e + k, 8, stride=0), :]
                acc[k] = acc[k] + s * jnp.concatenate([line] * (rows // 8), axis=0)
        if last:
            add_columns(gather, g * rows, rows, 4 * t, acc)
        else:
            for k in range(4):
                total[k, pl.ds(at, rows), :] = acc[k]


def atomic_phase(cells, first, last, lists, amat, bmat, rmat, dist0, dist1, total, gather):
    distances(0, cells, lists, amat, bmat, dist0)

    def two_tiles(p, _):
        t = 2 * p
        distances(t + 1, cells, lists, amat, bmat, dist1)
        accumulate(t, cells, first, last, lists, rmat, dist0, total, gather)
        distances(lax.rem(t + 2, 16), cells, lists, amat, bmat, dist0)
        accumulate(t + 1, cells, first, last, lists, rmat, dist1, total, gather)
        return 0

    lax.fori_loop(0, 8, two_tiles, 0)


def coarse_phase(lists, amat, bmat, rmat, wcol, dist0, gather):
    def one(b, _):
        a = amat[pl.ds(pl.multiple_of(2048 + b * 128, 128), 128), :]
        places = []
        for n in range(12):
            e = lists[0, 0, 0, b, n]
            places.append((e // 4) * TILES + 16 + e % 4)
        for n in range(0, 12, 2):
            tiles = [bmat[q // 2, q % 2] for q in places[n : n + 2]]
            dist0[:, n * 128 : n * 128 + 256] = dot_nn(a, jnp.concatenate(tiles, axis=1))
        rows = 32
        for g in range(128 // rows):
            acc = [jnp.zeros((rows, 128), f32) for _ in range(4)]
            own = wcol[pl.ds(pl.multiple_of(b * 128 + g * rows, rows), rows), :]
            for n in range(12):
                line = [
                    jnp.concatenate([rmat[pl.ds(4 * places[n] + k, 8, stride=0), :]] * (rows // 8), axis=0)
                    for k in range(4)
                ]
                d = dist0[g * rows : (g + 1) * rows, n * 128 : n * 128 + 128]
                s = jnp.exp(-inv_sigma_sq * d) * (1.0 - own * line[3])
                for k in range(3):
                    acc[k] = acc[k] + s * line[k]
                acc[3] = acc[3] + s
            add_columns(gather, g * rows, rows, 64 + 4 * b, acc)
        return 0

    lax.fori_loop(0, 4, one, 0)


def prologue(pos, charge, mass, weight, mapping, table, pay, wide16, bead16, beads):
    label = mapping[0, 0, 0:1, :]

    def rows_of_table(k, _):
        at = pl.multiple_of(k * 32, 32)
        ids = lax.broadcasted_iota(i32, (32, 2048), 0) + at
        table[pl.ds(at, 32), :] = jnp.where(ids == label, 1.0, 0.0).astype(bf16)
        return 0

    lax.fori_loop(0, 16, rows_of_table, 0)
    wide16[12:16, :] = jnp.zeros((4, 2048), f32)
    m = mass[0, 0, 0:1, :]
    for k in range(3):
        h, mid, l = split3(m * pos[0, 0, 0, k : k + 1, :])
        wide16[k : k + 1, :] = h
        wide16[4 + k : 5 + k, :] = mid
        wide16[8 + k : 9 + k, :] = l
    h, mid, l = split3(m)
    wide16[3:4, :] = h
    wide16[7:8, :] = mid
    wide16[11:12, :] = l
    bead16[...] = dot_nt(wide16[...].astype(bf16), table[...])
    sums = bead16[0:4, :] + bead16[4:8, :] + bead16[8:12, :]
    beads[0:3, :] = sums[0:3] / sums[3:4]
    beads[6:7, :] = weight[0, 0, 0:1, :]
    beads[7:8, :] = sums[3:4]
    bead16[...] = jnp.zeros((16, 512), f32)
    h, mid, l = split3(weight[0, 0, 0:1, :])
    bead16[0:1, :] = h
    bead16[1:2, :] = mid
    bead16[2:3, :] = l
    atom_weight = jnp.sum(dot_nn(bead16[...].astype(bf16), table[...]), axis=0, keepdims=True)
    qw = charge[0, 0, 0:1, :] * atom_weight
    for t in range(16):
        cut = slice(t * 128, t * 128 + 128)
        pay[OWN, 4 * t : 4 * t + 3, :] = pos[0, 0, 0, :, cut] - 0.5
        pay[OWN, 4 * t + 3 : 4 * t + 4, :] = qw[:, cut]
    for b in range(4):
        cut = slice(b * 128, b * 128 + 128)
        pay[OWN, 64 + 4 * b : 67 + 4 * b, :] = beads[0:3, cut] - 0.5
        pay[OWN, 67 + 4 * b : 68 + 4 * b, :] = weight[0, 0, 0:1, cut]


def epilogue(mass, leaving, table, pay, gather, flat, wide16, bead16, bead32, beads, forces, parcel):
    row, _ = place()
    own = pay[OWN].reshape(10, 8, 128)
    sums = gather[...].T[0:80, :].reshape(10, 8, 128)
    force = own * fourth_to_all(sums, row) - sums
    atomic = force[:8] * fourth_to_all(own[:8], row[:8])
    flat[...] = jnp.concatenate([atomic, 2.0 * force[8:]], axis=0).reshape(80, 128)
    bead16[...] = jnp.zeros((16, 512), f32)
    for b in range(4):
        cut = slice(b * 128, b * 128 + 128)
        bead16[0:3, cut] = flat[64 + 4 * b : 67 + 4 * b, :]
    h, m, l = split3(bead16[0:3, :] / beads[7:8, :])
    bead16[0:3, :] = h
    bead16[4:7, :] = m
    bead16[8:11, :] = l
    wide16[...] = dot_nn(bead16[...].astype(bf16), table[...])
    spread = (wide16[0:3, :] + wide16[4:7, :] + wide16[8:11, :]) * mass[0, 0, 0:1, :]
    for t in range(16):
        cut = slice(t * 128, t * 128 + 128)
        forces[0, 0, 0, :, cut] = flat[4 * t : 4 * t + 3, :] + spread[:, cut]
    h, m, l = split3(forces[0, 0, 0])
    wide16[...] = jnp.zeros((16, 2048), f32)
    wide16[0:3, :] = h
    wide16[4:7, :] = m
    wide16[8:11, :] = l
    bead16[...] = dot_nt(wide16[...].astype(bf16), table[...])
    beads[3:6, :] = bead16[0:3, :] + bead16[4:7, :] + bead16[8:11, :]
    h, m, l = split3(beads[...])
    bead32[0:8, :] = h
    bead32[8:16, :] = m
    bead32[16:24, :] = l
    bead32[24:32, :] = jnp.zeros((8, 512), f32)
    rows = bead32[...].astype(bf16)
    ids = lax.broadcasted_iota(i32, (512, 128), 0)
    for way in range(2):
        pick = jnp.where(ids == leaving[0, 0, 0, way : way + 1, :], 1.0, 0.0).astype(bf16)
        got = dot_nn(rows, pick)
        parcel[way] = got[0:8] + got[8:16] + got[16:24]


def body(
    comm,
    pos, charge, mass, weight, mapping, atom_lists, bead_lists, leaving, given,
    forces, arrivals,
    pay, bmat, rmat, amat, wcol, dist0, dist1, total, gather, table, wide16, bead16, bead32, beads, flat,
    parcel, landed, send_sem, recv_sem, pass_send, pass_recv,
):
    if comm:
        me = {a: lax.axis_index(a) for a in ("gx", "gy", "gz")}
        size = {a: lax.axis_size(a) for a in ("gx", "gy", "gz")}

        def at(axis, step):
            return tuple(
                lax.rem(me[a] + (size[a] + step), size[a]) if a == axis else me[a] for a in ("gx", "gy", "gz")
            )

        barrier = pltpu.get_barrier_semaphore()
        for axis in ("gx", "gy", "gz"):
            for step in (-1, 1):
                pl.semaphore_signal(barrier, inc=1, device_id=at(axis, step), device_id_type=MESH)

        copies = {}
        for s, (source, axis, step) in ROUTE.items():
            copies[s] = pltpu.make_async_remote_copy(
                src_ref=pay.at[source],
                dst_ref=pay.at[s],
                send_sem=send_sem.at[s],
                recv_sem=recv_sem.at[s],
                device_id=at(axis, step),
                device_id_type=MESH,
            )
    prologue(pos, charge, mass, weight, mapping, table, pay, wide16, bead16, beads)
    if comm:
        pl.semaphore_wait(barrier, 6)
        for s in WAVES[0]:
            copies[s].start()
    else:
        for s in ROUTE:
            pay[s] = given[s]
    gather[...] = jnp.zeros((128, 128), f32)
    build_own(pay, amat, wcol)
    build_cell(OWN, pay, bmat, rmat)
    shared = (atom_lists, amat, bmat, rmat, dist0, dist1, total, gather)
    atomic_phase([OWN], True, False, *shared)
    for w in range(3):
        if comm:
            for s in WAVES[w]:
                copies[s].wait_recv()
            if w < 2:
                for s in WAVES[w + 1]:
                    copies[s].start()
        for s in WAVES[w]:
            build_cell(s, pay, bmat, rmat)
        atomic_phase(WAVES[w], False, w == 2, *shared)
    coarse_phase(bead_lists, amat, bmat, rmat, wcol, dist0, gather)
    epilogue(mass, leaving, table, pay, gather, flat, wide16, bead16, bead32, beads, forces, parcel)
    if comm:
        passes = []
        for way, step in ((0, 1), (1, -1)):
            passes.append(
                pltpu.make_async_remote_copy(
                    src_ref=parcel.at[way],
                    dst_ref=landed.at[way],
                    send_sem=pass_send.at[way],
                    recv_sem=pass_recv.at[way],
                    device_id=at("gx", step),
                    device_id_type=MESH,
                )
            )
            passes[-1].start()
        for s in ROUTE:
            copies[s].wait_send()
        first = lax.broadcasted_iota(i32, (8, 128), 0) == 0
        for way, move in ((0, -1.0), (1, 1.0)):
            passes[way].wait_recv()
            arrivals[0, 0, 0, way] = landed[way] + jnp.where(first, move, 0.0)
        for way in range(2):
            passes[way].wait_send()
    else:
        arrivals[0, 0, 0] = parcel[...]


def make_kernel(comm):
    vmem = pl.BlockSpec(memory_space=pltpu.VMEM)
    smem = pl.BlockSpec(memory_space=pltpu.SMEM)
    specs = [vmem] * 5 + [smem] * 2 + [vmem]
    kernel = functools.partial(body, True) if comm else functools.partial(body, False)
    if comm:

        def kernel(*refs):
            body(True, *refs[:8], None, *refs[8:])

    else:
        specs = specs + [vmem]
    return pl.pallas_call(
        kernel,
        out_shape=(
            jax.ShapeDtypeStruct((1, 1, 1, 3, 2048), f32),
            jax.ShapeDtypeStruct((1, 1, 1, 2, 8, 128), f32),
        ),
        in_specs=specs,
        out_specs=(vmem, vmem),
        scratch_shapes=[
            pltpu.VMEM((27, 80, 128), f32),
            pltpu.VMEM((270, 2, 32, 128), bf16),
            pltpu.VMEM((27 * TILES * 4, 128), f32),
            pltpu.VMEM((TILES * 128, 32), bf16),
            pltpu.VMEM((512, 128), f32),
            pltpu.VMEM((128, 12 * 128), f32),
            pltpu.VMEM((128, 12 * 128), f32),
            pltpu.VMEM((4, 2048, 128), f32),
            pltpu.VMEM((128, 128), f32),
            pltpu.VMEM((512, 2048), bf16),
            pltpu.VMEM((16, 2048), f32),
            pltpu.VMEM((16, 512), f32),
            pltpu.VMEM((32, 512), f32),
            pltpu.VMEM((8, 512), f32),
            pltpu.VMEM((80, 128), f32),
            pltpu.VMEM((2, 8, 128), f32),
            pltpu.VMEM((2, 8, 128), f32),
            pltpu.SemaphoreType.DMA((27,)),
            pltpu.SemaphoreType.DMA((27,)),
            pltpu.SemaphoreType.DMA((2,)),
            pltpu.SemaphoreType.DMA((2,)),
        ],
        compiler_params=pltpu.CompilerParams(
            collective_id=0 if comm else None, has_side_effects=comm, vmem_limit_bytes=48 << 20
        ),
        name="force_step",
    )


def solution(mesh):
    def cell(*dims):
        return P("gx", "gy", "gz", *[None] * len(dims))

    placed = (cell(0, 0), cell(0), cell(0), cell(0), cell(0), cell(0, 0), cell(0, 0), cell(0, 0))
    return jax.shard_map(
        make_kernel(True),
        mesh=mesh,
        in_specs=placed,
        out_specs=(cell(0, 0), cell(0, 0, 0)),
        check_vma=False,
    )
```

time: 243 us -> 41.1 us (0.17)
  the two profiles are of different devices: /device:TPU:30 before, /device:TPU:2 now
where the time goes in v1:
time: 41.1 us; the launch traced here: 40.9 us
  Pallas kernels  38.1 us (93%)
  local copies, waits for them, and re-layouts  2.05 us (5%)
  between operations  0.75 us (2%)
    pallas_call x1, Pallas kernels  38.1 us
    unnamed x16, local copies, waits for them, and re-layouts  1.42 us

profile of v1, /device:TPU:2, one launch (start us, length us, event | category | flops | bytes accessed | tf_op | source)
XLA Modules:
  0.0 40.9 jit_solution(3650849896575188427)
XLA Ops:
  0.6 0.0 copy-start.6
  0.6 0.0 copy-start.5
  0.7 0.0 copy-start.3
  0.7 0.0 copy-start.2
  0.7 0.0 copy-start.4
  0.7 0.0 copy-start.1
  0.7 0.0 copy-start
  0.7 0.8 %copy.10.refs_0_ = f32[1,1,1,3,2048]{4,3,2,1,0:T(4,128)S(1)} copy(f32[1,1,1,3,2048]{4,2,3,1,0:T(1,128)} %param.8) | data formatting | bytes 49152 | tf_op args[0]
  1.5 0.0 copy-done.6
  1.5 0.0 copy-done.5
  1.5 0.0 copy-done.3
  1.5 0.0 copy-done.2
  1.5 0.0 copy-done.4
  1.5 0.0 copy-done.1
  1.6 0.0 copy-done
  1.6 38.1 %force_step.1 = (f32[1,1,1,3,2048]{4,3,2,1,0:T(4,128)S(1)}, f32[1,1,1,2,8,128]{5,4,3,2,1,0:T(8,128)S(1)}) custom-call(f32[1,1,1,3,2048]{4,3,2,1,0:T(4,128)S(1)} %copy.10.refs_0_, f32[1,1,1,2048]{3,2,1,0:T(1,128)S(1)} %copy-done, f32[1,1,1,2048]{3,2,1,0:T(1,128)S(1)} %copy-done.1, f32[1,1,1,512]{3,2,1,0:T(1,128)S(1)} %copy-done.4, ...), custom_call_target="tpu_custom_call" | custom-call | tf_op jit(solution)/shard_map/force_step/pallas_call
  39.7 0.6 %copy.11 = f32[1,1,1,3,2048]{4,2,3,1,0:T(1,128)} copy(f32[1,1,1,3,2048]{4,3,2,1,0:T(4,128)S(1)} %get-tuple-element.2) | data formatting | bytes 49152 | tf_op jit(solution)/shard_map/force_step/pallas_call
  40.3 0.6 %copy.13 = f32[1,1,1,2,8,128]{5,4,3,2,1,0:T(8,128)} copy(f32[1,1,1,2,8,128]{5,4,3,2,1,0:T(8,128)S(1)} %get-tuple-element.7) | data formatting | bytes 16384
Async XLA Ops:
  0.6 0.9 %copy-start.6 = (s32[1,1,1,2,128]{4,3,2,1,0:T(2,128)S(1)}, s32[1,1,1,2,128]{4,3,2,1,0:T(2,128)}, u32[]{:S(2)}) copy-start(s32[1,1,1,2,128]{4,3,2,1,0:T(2,128)} %refs_7_.1) | copy-start | bytes 3076
  0.6 0.9 %copy-start.5 = (s32[1,1,1,4,12]{4,3,2,1,0:T(4,128)S(1)}, s32[1,1,1,4,12]{4,3,2,1,0:T(4,128)}, u32[]{:S(2)}) copy-start(s32[1,1,1,4,12]{4,3,2,1,0:T(4,128)} %refs_6_.1) | copy-start | bytes 580
  0.7 0.9 %copy-start.3 = (s32[1,1,1,16,27]{4,3,2,1,0:T(8,128)S(1)}, s32[1,1,1,16,27]{4,3,2,1,0:T(8,128)}, u32[]{:S(2)}) copy-start(s32[1,1,1,16,27]{4,3,2,1,0:T(8,128)} %refs_5_.1) | copy-start | bytes 5188
  0.7 0.9 %copy-start.2 = (s32[1,1,1,2048]{3,2,1,0:T(1,128)S(1)}, s32[1,1,1,2048]{3,2,1,0:T(1,128)}, u32[]{:S(2)}) copy-start(s32[1,1,1,2048]{3,2,1,0:T(1,128)} %refs_4_.1) | copy-start | bytes 24580
  0.7 0.9 %copy-start.4 = (f32[1,1,1,512]{3,2,1,0:T(1,128)S(1)}, f32[1,1,1,512]{3,2,1,0:T(1,128)}, u32[]{:S(2)}) copy-start(f32[1,1,1,512]{3,2,1,0:T(1,128)} %refs_3_.1) | copy-start | bytes 6148
  0.7 0.9 %copy-start.1 = (f32[1,1,1,2048]{3,2,1,0:T(1,128)S(1)}, f32[1,1,1,2048]{3,2,1,0:T(1,128)}, u32[]{:S(2)}) copy-start(f32[1,1,1,2048]{3,2,1,0:T(1,128)} %refs_2_.1) | copy-start | bytes 24580
  0.7 0.9 %copy-start = (f32[1,1,1,2048]{3,2,1,0:T(1,128)S(1)}, f32[1,1,1,2048]{3,2,1,0:T(1,128)}, u32[]{:S(2)}) copy-start(f32[1,1,1,2048]{3,2,1,0:T(1,128)} %refs_1_.1) | copy-start | bytes 24580

commit v2 on v1

v2 whole, which is shorter than its diff:
```python
import functools

import jax
import jax.numpy as jnp
from jax import lax
from jax.experimental import pallas as pl
from jax.experimental.pallas import tpu as pltpu
from jax.sharding import PartitionSpec as P

soft_core = 0.01
inv_sigma_sq = 4.0
f32, bf16, i32 = jnp.float32, jnp.bfloat16, jnp.int32
MESH = pl.DeviceIdType.MESH
TILES = 20


def slot_of(a, b, c):
    return 9 * (a + 1) + 3 * (b + 1) + (c + 1)


OWN = slot_of(0, 0, 0)
PLANE = [(a, b) for a in (-1, 0, 1) for b in (-1, 0, 1) if a or b]
POLES = [slot_of(0, 0, c) for c in (-1, 1)]
SIDES = [slot_of(a, b, 0) for a, b in PLANE]
CORNERS = [slot_of(a, b, c) for a, b in PLANE for c in (-1, 1)]
ROUTE = {slot_of(0, 0, c): (0, 0, -c) for c in (-1, 1)}
ROUTE |= {slot_of(a, b, 0): (-a, -b, 0) for a, b in PLANE}
PARTNERS = [(0, 0, -1), (0, 0, 1)] + [(a, b, 0) for a, b in PLANE]


def split3(v):
    h = v.astype(bf16).astype(f32)
    r = v - h
    m = r.astype(bf16).astype(f32)
    return h, m, r - m


def dot_nt(a, b):
    return lax.dot_general(a, b, (((1,), (1,)), ((), ())), preferred_element_type=f32)


def dot_nn(a, b):
    return jnp.dot(a, b, preferred_element_type=f32)


def stack3(scr, rows, value):
    h, m, l = split3(value)
    scr[0:rows, :] = h
    scr[rows : 2 * rows, :] = m
    scr[2 * rows : 3 * rows, :] = l


def place():
    sub = lax.broadcasted_iota(i32, (10, 8, 128), 1)
    return sub & 3, sub < 4


def up_rows(x, by):
    return pltpu.roll(x, by % 8, 1)


def fourth_to_all(v, row):
    u = jnp.where(row == 3, v, 0.0)
    u = u + up_rows(u, -1)
    return u + up_rows(u, -2)


def squares_to_fourth(v):
    sq = v * v
    return up_rows(sq, 1) + up_rows(sq, 2) + up_rows(sq, 3)


def interleave(groups, low):
    even, odd = [], []
    for g, k in zip(groups[0::2], groups[1::2], strict=True):
        even.append(jnp.where(low, g, up_rows(k, 4)))
        odd.append(jnp.where(low, up_rows(g, 4), k))
    zero = jnp.zeros((10, 8, 128), f32)
    return (
        jnp.concatenate(even + [zero], axis=1),
        jnp.concatenate(odd + [zero], axis=1),
    )


def build_cell(slot, pay, bmat, rmat):
    row, low = place()
    v = pay[slot].reshape(10, 8, 128)
    offset = (slot // 9 - 1, slot // 3 % 3 - 1, slot % 3 - 1)
    for axis in range(3):
        if offset[axis]:
            v = v + jnp.where(row == axis, float(offset[axis]), 0.0)
    atoms, beads = v[:8], v[8:]
    scaled = jnp.where(row[:8] == 3, atoms, atoms * fourth_to_all(atoms, row[:8]))
    rmat[pl.ds(slot * TILES * 4, 64), :] = scaled.reshape(64, 128)
    rmat[pl.ds(slot * TILES * 4 + 64, 16), :] = beads.reshape(16, 128)
    h, m, l = split3(jnp.where(row == 3, squares_to_fourth(v), v))
    h1 = jnp.where(row == 3, 1.0, h)
    m1 = jnp.where(row == 3, 1.0, m)
    even, odd = interleave((h, h1, m, m1, l, h1), low)
    even, odd = even.astype(bf16), odd.astype(bf16)
    for k in range(10):
        bmat[slot * TILES + 2 * k] = even[k]
        bmat[slot * TILES + 2 * k + 1] = odd[k]


def build_own(pay, amat, wcol):
    row, low = place()
    v = pay[OWN].reshape(10, 8, 128)
    atom = lax.broadcasted_iota(i32, (10, 8, 128), 0) < 8
    near = squares_to_fourth(v) + jnp.where(atom, soft_core, 0.0)
    h, m, l = split3(jnp.where(row == 3, near, v))
    a0 = jnp.where(row == 3, 1.0, -2.0 * h)
    a1 = jnp.where(row == 3, h, -2.0 * m)
    a3 = jnp.where(row == 3, m, -2.0 * m)
    a5 = jnp.where(row == 3, l, -2.0 * l)
    even, odd = interleave((a0, a1, a0, a3, a0, a5), low)
    for t in range(TILES):
        half = (even, odd)[t % 2][t // 2]
        amat[t * 128 : t * 128 + 128, :] = half.T.astype(bf16)
    for b in range(4):
        r = 64 + 4 * b + 3
        wide = jnp.broadcast_to(pay[OWN, r : r + 1, :], (128, 128))
        wcol[b * 128 : b * 128 + 128, :] = wide.T


def distance(t, some, at, lists, amat, bmat, dist):
    a = amat[pl.ds(pl.multiple_of(t * 128, 128), 128), :]
    tiles = [bmat[lists[0, 0, 0, t, c] + 4 * c] for c in some]
    b = tiles[0] if len(some) == 1 else jnp.concatenate(tiles, axis=1)
    dist[:, at * 128 : (at + len(some)) * 128] = dot_nn(a, b)


def one_tile(t, ahead, now, later, cells, first, lists, amat, bmat, rmat, total, gather):
    rows, groups = 32, 4
    pairs = range(0, len(cells), 2)
    for g in range(groups):
        if gather is not None:
            add_up((t + 15) & 15, [g], total, gather)
        at = pl.multiple_of(t * 128 + g * rows, rows)
        if first:
            acc = [jnp.zeros((rows, 128), f32) for _ in range(4)]
        else:
            acc = [total[k, pl.ds(at, rows), :] for k in range(4)]
        for p in pairs:
            turn = g * len(pairs) + p // 2
            if turn % groups == 0:
                q = 2 * (turn // groups)
                distance(ahead, cells[q : q + 2], q, lists, amat, bmat, later)
            for n in range(p, min(p + 2, len(cells))):
                e = 4 * (lists[0, 0, 0, t, cells[n]] + 4 * cells[n])
                s = lax.rsqrt(now[g * rows : (g + 1) * rows, n * 128 : n * 128 + 128])
                s = s * s * s
                for k in range(4):
                    line = rmat[pl.ds(e + k, 8, stride=0), :]
                    acc[k] = acc[k] + s * jnp.concatenate([line] * (rows // 8), axis=0)
        for k in range(4):
            total[k, pl.ds(at, rows), :] = acc[k]


def add_columns(gather, rows, lane0, sums):
    lane = lax.broadcasted_iota(i32, (rows.size, 128), 1)
    got = gather[rows, :]
    for k in range(4):
        got = jnp.where(lane == lane0 + k, jnp.sum(sums[k], axis=1, keepdims=True), got)
    gather[rows, :] = got


def add_up(t, groups, total, gather):
    for g in groups:
        at = pl.ds(pl.multiple_of(t * 128 + g * 32, 32), 32)
        add_columns(gather, pl.ds(g * 32, 32), 4 * t, [total[k, at, :] for k in range(4)])


def abs_of(x):
    return jnp.maximum(x, -x)


def when(condition, work):
    if condition is True:
        work()
    else:
        pl.when(condition)(work)


def once(p, work):
    lax.fori_loop(0, 1 + jnp.minimum(p, 0), lambda _, c: (work(), c)[1], 0)


def atomic_phase(cells, first, lists, amat, bmat, rmat, dist0, dist1, total, gather=None):
    for q in range(0, len(cells), 2):
        distance(0, cells[q : q + 2], q, lists, amat, bmat, dist0)
    shared = (cells, first, lists, amat, bmat, rmat, total, gather)

    def two_tiles(p, _):
        once(p, lambda: one_tile(2 * p, 2 * p + 1, dist0, dist1, *shared))
        once(p, lambda: one_tile(2 * p + 1, (2 * p + 2) & 15, dist1, dist0, *shared))
        return 0

    lax.fori_loop(0, 8, two_tiles, 0)
    if gather is not None:
        add_up(15, range(4), total, gather)


def coarse_phase(lists, amat, bmat, rmat, wcol, dist0, gather):
    def one(b, _):
        a = amat[pl.ds(pl.multiple_of(2048 + b * 128, 128), 128), :]
        places = []
        for n in range(12):
            e = lists[0, 0, 0, b, n]
            places.append(16 * lax.shift_right_logical(e, 2) + e + 16)
        for n in range(0, 12, 2):
            tiles = [bmat[q] for q in places[n : n + 2]]
            dist0[:, n * 128 : n * 128 + 256] = dot_nn(a, jnp.concatenate(tiles, axis=1))
        rows = 32
        for g in range(128 // rows):
            acc = [jnp.zeros((rows, 128), f32) for _ in range(4)]
            own = wcol[pl.ds(pl.multiple_of(b * 128 + g * rows, rows), rows), :]
            for n in range(12):
                line = [
                    jnp.concatenate([rmat[pl.ds(4 * places[n] + k, 8, stride=0), :]] * (rows // 8), axis=0)
                    for k in range(4)
                ]
                d = dist0[g * rows : (g + 1) * rows, n * 128 : n * 128 + 128]
                s = jnp.exp(-inv_sigma_sq * d) * (1.0 - own * line[3])
                for k in range(3):
                    acc[k] = acc[k] + s * line[k]
                acc[3] = acc[3] + s
            add_columns(gather, pl.ds(g * rows, rows), 64 + 4 * b, acc)
        return 0

    lax.fori_loop(0, 4, one, 0)


def prologue(pos, charge, mass, weight, mapping, table, pay, wide16, bead16, beads):
    label = mapping[0, 0, 0:1, :]

    def rows_of_table(k, _):
        at = pl.multiple_of(k * 32, 32)
        ids = lax.broadcasted_iota(i32, (32, 2048), 0) + at
        table[pl.ds(at, 32), :] = jnp.where(ids == label, 1.0, 0.0).astype(bf16)
        return 0

    lax.fori_loop(0, 16, rows_of_table, 0)
    wide16[12:16, :] = jnp.zeros((4, 2048), f32)
    m = mass[0, 0, 0:1, :]
    for k in range(3):
        h, mid, l = split3(m * pos[0, 0, k, 0:1, :])
        wide16[k : k + 1, :] = h
        wide16[4 + k : 5 + k, :] = mid
        wide16[8 + k : 9 + k, :] = l
    h, mid, l = split3(m)
    wide16[3:4, :] = h
    wide16[7:8, :] = mid
    wide16[11:12, :] = l
    bead16[...] = dot_nt(wide16[...].astype(bf16), table[...])
    sums = bead16[0:4, :] + bead16[4:8, :] + bead16[8:12, :]
    beads[0:3, :] = sums[0:3] / sums[3:4]
    beads[6:7, :] = weight[0, 0, 0:1, :]
    beads[7:8, :] = sums[3:4]
    bead16[...] = jnp.zeros((16, 512), f32)
    h, mid, l = split3(weight[0, 0, 0:1, :])
    bead16[0:1, :] = h
    bead16[1:2, :] = mid
    bead16[2:3, :] = l
    atom_weight = jnp.sum(dot_nn(bead16[...].astype(bf16), table[...]), axis=0, keepdims=True)
    qw = charge[0, 0, 0:1, :] * atom_weight
    for t in range(16):
        cut = slice(t * 128, t * 128 + 128)
        for k in range(3):
            pay[OWN, 4 * t + k : 4 * t + k + 1, :] = pos[0, 0, k, 0:1, cut] - 0.5
        pay[OWN, 4 * t + 3 : 4 * t + 4, :] = qw[:, cut]
    for b in range(4):
        cut = slice(b * 128, b * 128 + 128)
        pay[OWN, 64 + 4 * b : 67 + 4 * b, :] = beads[0:3, cut] - 0.5
        pay[OWN, 67 + 4 * b : 68 + 4 * b, :] = weight[0, 0, 0:1, cut]


def epilogue(leaving, table, pay, gather, flat, flat3, wide16, bead16, bead32, beads, parcel):
    row, _ = place()
    own = pay[OWN].reshape(10, 8, 128)
    summed = gather[...].T[0:80, :].reshape(10, 8, 128)
    force = own * fourth_to_all(summed, row) - summed
    atomic = force[:8] * fourth_to_all(own[:8], row[:8])
    flat[...] = jnp.concatenate([atomic, 2.0 * force[8:]], axis=0).reshape(80, 128)
    for b in range(4):
        beads[3:6, b * 128 : b * 128 + 128] = flat[64 + 4 * b : 67 + 4 * b, :]
    h, m, l = split3(beads[3:6, :] / beads[7:8, :])
    bead16[...] = jnp.zeros((16, 512), f32)
    bead16[0:3, :] = h
    bead16[4:7, :] = m
    bead16[8:11, :] = l
    coarse = bead16[...].astype(bf16)
    h, m, l = split3(atomic.reshape(64, 128))
    wide16[12:16, :] = jnp.zeros((4, 2048), f32)
    flat3[0] = h
    flat3[1] = m
    flat3[2] = l
    for t in range(16):
        cut = slice(t * 128, t * 128 + 128)
        for k in range(3):
            wide16[4 * k : 4 * k + 4, cut] = flat3[k, 4 * t : 4 * t + 4, :]
    bead16[...] = dot_nt(wide16[...].astype(bf16), table[...])
    beads[3:6, :] = beads[3:6, :] + (bead16[0:3, :] + bead16[4:7, :] + bead16[8:11, :])
    h, m, l = split3(beads[...])
    bead32[0:8, :] = h
    bead32[8:16, :] = m
    bead32[16:24, :] = l
    bead32[24:32, :] = jnp.zeros((8, 512), f32)
    rows = bead32[...].astype(bf16)
    ids = lax.broadcasted_iota(i32, (512, 128), 0)
    for way in range(2):
        pick = jnp.where(ids == leaving[0, 0, 0, way : way + 1, :], 1.0, 0.0).astype(bf16)
        got = dot_nn(rows, pick)
        parcel[way] = got[0:8] + got[8:16] + got[16:24]
    return coarse


def finish(mass, table, coarse, flat, wide16, forces):
    wide16[...] = dot_nn(coarse, table[...])
    spread = (wide16[0:3, :] + wide16[4:7, :] + wide16[8:11, :]) * mass[0, 0, 0:1, :]
    for t in range(16):
        cut = slice(t * 128, t * 128 + 128)
        got = flat[4 * t : 4 * t + 3, :] + spread[:, cut]
        for k in range(3):
            forces[0, 0, k, 0:1, cut] = got[k : k + 1]


def body(comm, *refs):
    inputs, refs = refs[:8], refs[8:]
    if not comm:
        given, refs = refs[0], refs[1:]
    (
        forces, arrivals, pos, charge, mass, weight, mapping, atom_lists, bead_lists, leaving,
        pay, bmat, rmat, amat, wcol, dist0, dist1, total, gather, table, wide16, bead16, bead32, beads, flat, flat3,
        parcel, landed, load_sem, send_sem, recv_sem, pass_send, pass_recv,
    ) = refs
    staged = (pos, charge, mass, weight, mapping, atom_lists, bead_lists, leaving)
    loads = [pltpu.make_async_copy(inputs[n], staged[n], load_sem.at[n]) for n in range(8)]
    for n in (4, 3, 2, 0, 1, 5, 6, 7):
        loads[n].start()
    if comm:
        axes = ("gx", "gy", "gz")
        me = [lax.axis_index(a) for a in axes]
        size = [lax.axis_size(a) for a in axes]

        def at(steps):
            return tuple(lax.rem(me[n] + (size[n] + steps[n]), size[n]) if steps[n] else me[n] for n in range(3))

        barrier = pltpu.get_barrier_semaphore()
        for steps in PARTNERS:
            pl.semaphore_signal(barrier, inc=1, device_id=at(steps), device_id_type=MESH)

        def send(source, target, sem, steps):
            return pltpu.make_async_remote_copy(
                src_ref=pay.at[source],
                dst_ref=pay.at[target],
                send_sem=send_sem.at[sem],
                recv_sem=recv_sem.at[sem],
                device_id=at(steps),
                device_id_type=MESH,
            )

        copies = {s: send(OWN, s, s, steps) for s, steps in ROUTE.items()}
        near = 1 - 2 * lax.rem(me[2], 2)
        other = (me[0], me[1], me[2] + near)
        far_copies, near_copies, near_arrivals = [], [], []
        for a, b in PLANE:
            side = slot_of(a, b, 0)
            far_copies.append(send(OWN - near, side - near, side - 1, (-a, -b, 0)))
            for target, group in ((side - near, near_copies), (side + near, near_arrivals)):
                group.append(
                    pltpu.make_async_remote_copy(
                        src_ref=pay.at[side],
                        dst_ref=pay.at[target],
                        send_sem=send_sem.at[side + 1],
                        recv_sem=recv_sem.at[side + 1],
                        device_id=other,
                        device_id_type=MESH,
                    )
                )
    if comm:
        away = abs_of(2 * me[0] + 1 - size[0])
        has_atomic = 10 * away < 7 * size[0]
        has_coarse = 10 * (away + 2) >= 3 * size[0]
    else:
        has_atomic = has_coarse = True
    for n in range(8):
        loads[n].wait()
    prologue(pos, charge, mass, weight, mapping, table, pay, wide16, bead16, beads)
    if comm:
        pl.semaphore_wait(barrier, len(PARTNERS))
        for s in POLES + SIDES:
            copies[s].start()
    else:
        for s in POLES + SIDES + CORNERS:
            pay[s] = given[s]
    build_own(pay, amat, wcol)
    build_cell(OWN, pay, bmat, rmat)
    shared = (atom_lists, amat, bmat, rmat, dist0, dist1, total)
    gather[...] = jnp.zeros((128, 128), f32)
    when(has_atomic, lambda: atomic_phase([OWN], True, *shared))
    if comm:
        for s in POLES:
            copies[s].wait_recv()
        for copy in far_copies:
            copy.start()
    for s in POLES:
        build_cell(s, pay, bmat, rmat)
    when(has_atomic, lambda: atomic_phase(POLES, False, *shared))
    if comm:
        for s in SIDES:
            copies[s].wait_recv()
        for copy in near_copies:
            copy.start()
    for s in SIDES:
        build_cell(s, pay, bmat, rmat)
    when(has_atomic, lambda: atomic_phase(SIDES, False, *shared))
    if comm:
        for copy in far_copies + near_arrivals:
            copy.wait_recv()
    for s in CORNERS:
        build_cell(s, pay, bmat, rmat)
    when(has_atomic, lambda: atomic_phase(CORNERS, False, *shared, gather))
    when(has_coarse, lambda: coarse_phase(bead_lists, amat, bmat, rmat, wcol, dist0, gather))
    coarse = epilogue(leaving, table, pay, gather, flat, flat3, wide16, bead16, bead32, beads, parcel)
    if comm:
        passes = []
        for way, step in ((0, 1), (1, -1)):
            passes.append(
                pltpu.make_async_remote_copy(
                    src_ref=parcel.at[way],
                    dst_ref=landed.at[way],
                    send_sem=pass_send.at[way],
                    recv_sem=pass_recv.at[way],
                    device_id=at((step, 0, 0)),
                    device_id_type=MESH,
                )
            )
            passes[-1].start()
        finish(mass, table, coarse, flat, wide16, forces)
        for copy in [*copies.values(), *far_copies, *near_copies]:
            copy.wait_send()
        first = lax.broadcasted_iota(i32, (8, 128), 0) == 0
        for way, move in ((0, -1.0), (1, 1.0)):
            passes[way].wait_recv()
            arrivals[0, 0, 0, way] = landed[way] + jnp.where(first, move, 0.0)
        for way in range(2):
            passes[way].wait_send()
    else:
        finish(mass, table, coarse, flat, wide16, forces)
        arrivals[0, 0, 0] = parcel[...]


def make_kernel(comm):
    vmem = pl.BlockSpec(memory_space=pltpu.VMEM)
    specs = [pl.BlockSpec(memory_space=pltpu.HBM)] * 8 + ([] if comm else [vmem])
    return pl.pallas_call(
        functools.partial(body, comm),
        out_shape=(
            jax.ShapeDtypeStruct((1, 1, 3, 1, 2048), f32),
            jax.ShapeDtypeStruct((1, 1, 1, 2, 8, 128), f32),
        ),
        in_specs=specs,
        out_specs=(vmem, vmem),
        scratch_shapes=[
            pltpu.VMEM((1, 1, 3, 1, 2048), f32),
            pltpu.VMEM((1, 1, 1, 2048), f32),
            pltpu.VMEM((1, 1, 1, 2048), f32),
            pltpu.VMEM((1, 1, 1, 512), f32),
            pltpu.VMEM((1, 1, 1, 2048), i32),
            pltpu.SMEM((1, 1, 1, 16, 27), i32),
            pltpu.SMEM((1, 1, 1, 4, 12), i32),
            pltpu.VMEM((1, 1, 1, 2, 128), i32),
            pltpu.VMEM((27, 80, 128), f32),
            pltpu.VMEM((27 * TILES, 32, 128), bf16),
            pltpu.VMEM((27 * TILES * 4, 128), f32),
            pltpu.VMEM((TILES * 128, 32), bf16),
            pltpu.VMEM((512, 128), f32),
            pltpu.VMEM((128, 16 * 128), f32),
            pltpu.VMEM((128, 16 * 128), f32),
            pltpu.VMEM((4, 2048, 128), f32),
            pltpu.VMEM((128, 128), f32),
            pltpu.VMEM((512, 2048), bf16),
            pltpu.VMEM((16, 2048), f32),
            pltpu.VMEM((16, 512), f32),
            pltpu.VMEM((32, 512), f32),
            pltpu.VMEM((8, 512), f32),
            pltpu.VMEM((80, 128), f32),
            pltpu.VMEM((3, 64, 128), f32),
            pltpu.VMEM((2, 8, 128), f32),
            pltpu.VMEM((2, 8, 128), f32),
            pltpu.SemaphoreType.DMA((8,)),
            pltpu.SemaphoreType.DMA((27,)),
            pltpu.SemaphoreType.DMA((27,)),
            pltpu.SemaphoreType.DMA((2,)),
            pltpu.SemaphoreType.DMA((2,)),
        ],
        compiler_params=pltpu.CompilerParams(
            collective_id=0 if comm else None, has_side_effects=comm, vmem_limit_bytes=48 << 20
        ),
        name="force_step",
    )


def solution(mesh):
    def cell(*dims):
        return P("gx", "gy", "gz", *[None] * len(dims))

    placed = (cell(0, 0), cell(0), cell(0), cell(0), cell(0), cell(0, 0), cell(0, 0), cell(0, 0))
    def step(positions, *rest):
        operands = [pltpu.with_memory_space_constraint(x, pltpu.HBM) for x in (jnp.swapaxes(positions, 2, 3), *rest)]
        forces, arrivals = make_kernel(True)(*operands)
        return jnp.swapaxes(forces, 2, 3), arrivals

    return jax.shard_map(
        step,
        mesh=mesh,
        in_specs=placed,
        out_specs=(cell(0, 0), cell(0, 0, 0)),
        check_vma=False,
    )
```

time: 41.1 us -> 36.3 us (0.88)
  the two profiles are of different devices: /device:TPU:2 before, /device:TPU:65 now
where the time goes in v2:
time: 36.3 us; the launch traced here: 36.1 us
  Pallas kernels  34.3 us (94%)
  local copies, waits for them, and re-layouts  1.21 us (3%)
  between operations  0.64 us (2%)
    pallas_call x1, Pallas kernels, step(): forces, arrivals = make_kernel(True)(*operands)  34.3 us
    unnamed x2, local copies, waits for them, and re-layouts  1.21 us

profile of v2, /device:TPU:65, one launch (start us, length us, event | category | flops | bytes accessed | tf_op | source)
XLA Modules:
  0.0 36.1 jit_solution(14587827661887480626)
XLA Ops:
  0.6 34.3 %force_step.1 = (f32[1,1,3,1,2048]{4,3,2,1,0:T(1,128)S(1)}, f32[1,1,1,2,8,128]{5,4,3,2,1,0:T(8,128)S(1)}) custom-call(f32[1,1,3,1,2048]{4,3,2,1,0:T(1,128)} %bitcast.5, f32[1,1,1,2048]{3,2,1,0:T(1,128)} %refs_1_.1, f32[1,1,1,2048]{3,2,1,0:T(1,128)} %refs_2_.1, f32[1,1,1,512]{3,2,1,0:T(1,128)} %refs_3_.1, s32[1,1,1,2048]{3,2,1,0:T(1,128)} %refs_4_.1, ...), custom_call_target="tpu_custom_call" | custom-call | tf_op jit(solution)/shard_map/force_step/pallas_call | solution.py:512
  34.9 0.6 %copy.13 = f32[1,1,1,3,2048]{4,2,3,1,0:T(1,128)} copy(f32[1,1,1,3,2048]{4,2,3,1,0:T(1,128)S(1)} %bitcast.4) | data formatting | bytes 49152
  35.5 0.6 %copy.14 = f32[1,1,1,2,8,128]{5,4,3,2,1,0:T(8,128)} copy(f32[1,1,1,2,8,128]{5,4,3,2,1,0:T(8,128)S(1)} %get-tuple-element.11) | data formatting | bytes 16384

commit v3 on v2

--- a/solution.py
+++ b/solution.py
@@ -9,6 +9,7 @@
 
 soft_core = 0.01
 inv_sigma_sq = 4.0
+log2_e = 1.4426950408889634
 f32, bf16, i32 = jnp.float32, jnp.bfloat16, jnp.int32
 MESH = pl.DeviceIdType.MESH
 TILES = 20
@@ -130,12 +131,12 @@
     dist[:, at * 128 : (at + len(some)) * 128] = dot_nn(a, b)
 
 
-def one_tile(t, ahead, now, later, cells, first, lists, amat, bmat, rmat, total, gather):
+def one_tile(t, ahead, now, later, cells, first, lists, amat, bmat, rmat, total, gather, before=None, done=None):
     rows, groups = 32, 4
     pairs = range(0, len(cells), 2)
     for g in range(groups):
         if gather is not None:
-            add_up((t + 15) & 15, [g], total, gather)
+            add_up((t + 15) & 15, [g], before, gather)
         at = pl.multiple_of(t * 128 + g * rows, rows)
         if first:
             acc = [jnp.zeros((rows, 128), f32) for _ in range(4)]
@@ -154,7 +155,10 @@
                     line = rmat[pl.ds(e + k, 8, stride=0), :]
                     acc[k] = acc[k] + s * jnp.concatenate([line] * (rows // 8), axis=0)
         for k in range(4):
-            total[k, pl.ds(at, rows), :] = acc[k]
+            if done is None:
+                total[k, pl.ds(at, rows), :] = acc[k]
+            else:
+                done[k, g * rows : (g + 1) * rows, :] = acc[k]
 
 
 def add_columns(gather, rows, lane0, sums):
@@ -165,10 +169,10 @@
     gather[rows, :] = got
 
 
-def add_up(t, groups, total, gather):
+def add_up(t, groups, done, gather):
     for g in groups:
-        at = pl.ds(pl.multiple_of(t * 128 + g * 32, 32), 32)
-        add_columns(gather, pl.ds(g * 32, 32), 4 * t, [total[k, at, :] for k in range(4)])
+        at = pl.ds(g * 32, 32)
+        add_columns(gather, at, 4 * t, [done[k, at, :] for k in range(4)])
 
 
 def abs_of(x):
@@ -186,58 +190,68 @@
     lax.fori_loop(0, 1 + jnp.minimum(p, 0), lambda _, c: (work(), c)[1], 0)
 
 
-def atomic_phase(cells, first, lists, amat, bmat, rmat, dist0, dist1, total, gather=None):
+def atomic_phase(cells, first, lists, amat, bmat, rmat, dist0, dist1, total, gather=None, done=(None, None)):
     for q in range(0, len(cells), 2):
         distance(0, cells[q : q + 2], q, lists, amat, bmat, dist0)
     shared = (cells, first, lists, amat, bmat, rmat, total, gather)
 
     def two_tiles(p, _):
-        once(p, lambda: one_tile(2 * p, 2 * p + 1, dist0, dist1, *shared))
-        once(p, lambda: one_tile(2 * p + 1, (2 * p + 2) & 15, dist1, dist0, *shared))
+        once(p, lambda: one_tile(2 * p, 2 * p + 1, dist0, dist1, *shared, done[1], done[0]))
+        once(p, lambda: one_tile(2 * p + 1, (2 * p + 2) & 15, dist1, dist0, *shared, done[0], done[1]))
         return 0
 
     lax.fori_loop(0, 8, two_tiles, 0)
     if gather is not None:
-        add_up(15, range(4), total, gather)
-
-
-def coarse_phase(lists, amat, bmat, rmat, wcol, dist0, gather):
-    def one(b, _):
-        a = amat[pl.ds(pl.multiple_of(2048 + b * 128, 128), 128), :]
-        places = []
+        add_up(15, range(4), done[1], gather)
+
+
+def bead_places(lists, b):
+    return [16 * lax.shift_right_logical(lists[0, 0, 0, b, n], 2) + lists[0, 0, 0, b, n] + 16 for n in range(12)]
+
+
+def bead_distances(b, n, lists, amat, bmat, dist):
+    a = amat[2048 + b * 128 : 2176 + b * 128, :]
+    tiles = [bmat[q] for q in bead_places(lists, b)[n : n + 2]]
+    dist[:, n * 128 : n * 128 + 256] = dot_nn(a, jnp.concatenate(tiles, axis=1))
+
+
+def bead_tile(b, now, later, lists, amat, bmat, rmat, wcol, gather):
+    rows = 32
+    places = bead_places(lists, b)
+    for g in range(128 // rows):
+        acc = [jnp.zeros((rows, 128), f32) for _ in range(4)]
+        own = wcol[b * 128 + g * rows : b * 128 + (g + 1) * rows, :]
         for n in range(12):
-            e = lists[0, 0, 0, b, n]
-            places.append(16 * lax.shift_right_logical(e, 2) + e + 16)
-        for n in range(0, 12, 2):
-            tiles = [bmat[q] for q in places[n : n + 2]]
-            dist0[:, n * 128 : n * 128 + 256] = dot_nn(a, jnp.concatenate(tiles, axis=1))
-        rows = 32
-        for g in range(128 // rows):
-            acc = [jnp.zeros((rows, 128), f32) for _ in range(4)]
-            own = wcol[pl.ds(pl.multiple_of(b * 128 + g * rows, rows), rows), :]
-            for n in range(12):
-                line = [
-                    jnp.concatenate([rmat[pl.ds(4 * places[n] + k, 8, stride=0), :]] * (rows // 8), axis=0)
-                    for k in range(4)
-                ]
-                d = dist0[g * rows : (g + 1) * rows, n * 128 : n * 128 + 128]
-                s = jnp.exp(-inv_sigma_sq * d) * (1.0 - own * line[3])
-                for k in range(3):
-                    acc[k] = acc[k] + s * line[k]
-                acc[3] = acc[3] + s
-            add_columns(gather, pl.ds(g * rows, rows), 64 + 4 * b, acc)
-        return 0
-
-    lax.fori_loop(0, 4, one, 0)
-
-
-def prologue(pos, charge, mass, weight, mapping, table, pay, wide16, bead16, beads):
+            if b < 3 and n % 2 == 0 and (6 * g + n // 2) % 4 == 0:
+                bead_distances(b + 1, 2 * ((6 * g + n // 2) // 4), lists, amat, bmat, later)
+            line = [
+                jnp.concatenate([rmat[pl.ds(4 * places[n] + k, 8, stride=0), :]] * (rows // 8), axis=0) for k in range(4)
+            ]
+            d = now[g * rows : (g + 1) * rows, n * 128 : n * 128 + 128]
+            s = jnp.exp2((-inv_sigma_sq * log2_e) * d) * (1.0 - own * line[3])
+            for k in range(3):
+                acc[k] = acc[k] + s * line[k]
+            acc[3] = acc[3] + s
+        add_columns(gather, pl.ds(g * rows, rows), 64 + 4 * b, acc)
+
+
+def coarse_phase(lists, amat, bmat, rmat, wcol, dist0, dist1, gather):
+    for n in range(0, 12, 2):
+        bead_distances(0, n, lists, amat, bmat, dist0)
+    for b in range(4):
+        bead_tile(b, (dist0, dist1)[b % 2], (dist1, dist0)[b % 2], lists, amat, bmat, rmat, wcol, gather)
+
+
+def prologue(pos, charge, mass, weight, mapping, table, pay, wide16, bead16, light16, beads):
     label = mapping[0, 0, 0:1, :]
+
+    label16 = label.astype(jnp.int16)
 
     def rows_of_table(k, _):
         at = pl.multiple_of(k * 32, 32)
-        ids = lax.broadcasted_iota(i32, (32, 2048), 0) + at
-        table[pl.ds(at, 32), :] = jnp.where(ids == label, 1.0, 0.0).astype(bf16)
+        ids = (lax.broadcasted_iota(i32, (32, 2048), 0) + at).astype(jnp.int16)
+        same = ids == jnp.broadcast_to(label16, (32, 2048))
+        table[pl.ds(at, 32), :] = jnp.where(same, jnp.ones((), bf16), jnp.zeros((), bf16))
         return 0
 
     lax.fori_loop(0, 16, rows_of_table, 0)
@@ -257,12 +271,12 @@
     beads[0:3, :] = sums[0:3] / sums[3:4]
     beads[6:7, :] = weight[0, 0, 0:1, :]
     beads[7:8, :] = sums[3:4]
-    bead16[...] = jnp.zeros((16, 512), f32)
+    light16[...] = jnp.zeros((16, 512), f32)
     h, mid, l = split3(weight[0, 0, 0:1, :])
-    bead16[0:1, :] = h
-    bead16[1:2, :] = mid
-    bead16[2:3, :] = l
-    atom_weight = jnp.sum(dot_nn(bead16[...].astype(bf16), table[...]), axis=0, keepdims=True)
+    light16[0:1, :] = h
+    light16[1:2, :] = mid
+    light16[2:3, :] = l
+    atom_weight = jnp.sum(dot_nn(light16[...].astype(bf16), table[...]), axis=0, keepdims=True)
     qw = charge[0, 0, 0:1, :] * atom_weight
     for t in range(16):
         cut = slice(t * 128, t * 128 + 128)
@@ -275,44 +289,54 @@
         pay[OWN, 67 + 4 * b : 68 + 4 * b, :] = weight[0, 0, 0:1, cut]
 
 
-def epilogue(leaving, table, pay, gather, flat, flat3, wide16, bead16, bead32, beads, parcel):
+def build_leavers(leaving, mapping, picks, leavers):
+    ids = lax.broadcasted_iota(i32, (512, 128), 0)
+    for way in range(2):
+        row = leaving[0, 0, 0, way : way + 1, :]
+        picks[:, way * 128 : way * 128 + 128] = jnp.where(ids == row, 1.0, 0.0).astype(bf16)
+        column = jnp.broadcast_to(row.astype(f32), (128, 128)).T.astype(i32)
+        for t in range(16):
+            cut = slice(t * 128, t * 128 + 128)
+            leavers[way * 128 : way * 128 + 128, cut] = jnp.where(column == mapping[0, 0, 0:1, cut], 1.0, 0.0).astype(bf16)
+
+
+def epilogue(pay, gather, picks, leavers, flat, flat3, wide16, bead16, bead32, beads, parcel):
     row, _ = place()
     own = pay[OWN].reshape(10, 8, 128)
     summed = gather[...].T[0:80, :].reshape(10, 8, 128)
     force = own * fourth_to_all(summed, row) - summed
     atomic = force[:8] * fourth_to_all(own[:8], row[:8])
     flat[...] = jnp.concatenate([atomic, 2.0 * force[8:]], axis=0).reshape(80, 128)
+    h, m, l = split3(atomic.reshape(64, 128))
+    flat3[0] = h
+    flat3[1] = m
+    flat3[2] = l
+    wide16[12:16, :] = jnp.zeros((4, 2048), f32)
+    for t in range(16):
+        cut = slice(t * 128, t * 128 + 128)
+        for k in range(3):
+            wide16[4 * k : 4 * k + 4, cut] = flat3[k, 4 * t : 4 * t + 4, :]
+    summed = dot_nt(wide16[...].astype(bf16), leavers[...])
     for b in range(4):
         beads[3:6, b * 128 : b * 128 + 128] = flat[64 + 4 * b : 67 + 4 * b, :]
+    h, m, l = split3(beads[...])
+    bead32[0:8, :] = h
+    bead32[8:16, :] = m
+    bead32[16:24, :] = l
+    bead32[24:32, :] = jnp.zeros((8, 512), f32)
+    got = dot_nn(bead32[...].astype(bf16), picks[...])
+    got = got[0:8] + got[8:16] + got[16:24]
+    bead16[:, 0:256] = summed
+    for way in range(2):
+        cut = slice(way * 128, way * 128 + 128)
+        parcel[way] = got[:, cut]
+        parcel[way, 3:6, :] = parcel[way, 3:6, :] + (bead16[0:3, cut] + bead16[4:7, cut] + bead16[8:11, cut])
     h, m, l = split3(beads[3:6, :] / beads[7:8, :])
     bead16[...] = jnp.zeros((16, 512), f32)
     bead16[0:3, :] = h
     bead16[4:7, :] = m
     bead16[8:11, :] = l
-    coarse = bead16[...].astype(bf16)
-    h, m, l = split3(atomic.reshape(64, 128))
-    wide16[12:16, :] = jnp.zeros((4, 2048), f32)
-    flat3[0] = h
-    flat3[1] = m
-    flat3[2] = l
-    for t in range(16):
-        cut = slice(t * 128, t * 128 + 128)
-        for k in range(3):
-            wide16[4 * k : 4 * k + 4, cut] = flat3[k, 4 * t : 4 * t + 4, :]
-    bead16[...] = dot_nt(wide16[...].astype(bf16), table[...])
-    beads[3:6, :] = beads[3:6, :] + (bead16[0:3, :] + bead16[4:7, :] + bead16[8:11, :])
-    h, m, l = split3(beads[...])
-    bead32[0:8, :] = h
-    bead32[8:16, :] = m
-    bead32[16:24, :] = l
-    bead32[24:32, :] = jnp.zeros((8, 512), f32)
-    rows = bead32[...].astype(bf16)
-    ids = lax.broadcasted_iota(i32, (512, 128), 0)
-    for way in range(2):
-        pick = jnp.where(ids == leaving[0, 0, 0, way : way + 1, :], 1.0, 0.0).astype(bf16)
-        got = dot_nn(rows, pick)
-        parcel[way] = got[0:8] + got[8:16] + got[16:24]
-    return coarse
+    return bead16[...].astype(bf16)
 
 
 def finish(mass, table, coarse, flat, wide16, forces):
@@ -331,7 +355,7 @@
         given, refs = refs[0], refs[1:]
     (
         forces, arrivals, pos, charge, mass, weight, mapping, atom_lists, bead_lists, leaving,
-        pay, bmat, rmat, amat, wcol, dist0, dist1, total, gather, table, wide16, bead16, bead32, beads, flat, flat3,
+        pay, bmat, rmat, amat, wcol, dist0, dist1, done0, done1, total, gather, table, wide16, bead16, light16, bead32, beads, picks, leavers, flat, flat3,
         parcel, landed, load_sem, send_sem, recv_sem, pass_send, pass_recv,
     ) = refs
     staged = (pos, charge, mass, weight, mapping, atom_lists, bead_lists, leaving)
@@ -386,7 +410,7 @@
         has_atomic = has_coarse = True
     for n in range(8):
         loads[n].wait()
-    prologue(pos, charge, mass, weight, mapping, table, pay, wide16, bead16, beads)
+    prologue(pos, charge, mass, weight, mapping, table, pay, wide16, bead16, light16, beads)
     if comm:
         pl.semaphore_wait(barrier, len(PARTNERS))
         for s in POLES + SIDES:
@@ -395,6 +419,7 @@
         for s in POLES + SIDES + CORNERS:
             pay[s] = given[s]
     build_own(pay, amat, wcol)
+    build_leavers(leaving, mapping, picks, leavers)
     build_cell(OWN, pay, bmat, rmat)
     shared = (atom_lists, amat, bmat, rmat, dist0, dist1, total)
     gather[...] = jnp.zeros((128, 128), f32)
@@ -420,9 +445,9 @@
             copy.wait_recv()
     for s in CORNERS:
         build_cell(s, pay, bmat, rmat)
-    when(has_atomic, lambda: atomic_phase(CORNERS, False, *shared, gather))
-    when(has_coarse, lambda: coarse_phase(bead_lists, amat, bmat, rmat, wcol, dist0, gather))
-    coarse = epilogue(leaving, table, pay, gather, flat, flat3, wide16, bead16, bead32, beads, parcel)
+    when(has_atomic, lambda: atomic_phase(CORNERS, False, *shared, gather, (done0, done1)))
+    when(has_coarse, lambda: coarse_phase(bead_lists, amat, bmat, rmat, wcol, dist0, dist1, gather))
+    coarse = epilogue(pay, gather, picks, leavers, flat, flat3, wide16, bead16, bead32, beads, parcel)
     if comm:
         passes = []
         for way, step in ((0, 1), (1, -1)):
@@ -478,13 +503,18 @@
             pltpu.VMEM((512, 128), f32),
             pltpu.VMEM((128, 16 * 128), f32),
             pltpu.VMEM((128, 16 * 128), f32),
+            pltpu.VMEM((4, 128, 128), f32),
+            pltpu.VMEM((4, 128, 128), f32),
             pltpu.VMEM((4, 2048, 128), f32),
             pltpu.VMEM((128, 128), f32),
             pltpu.VMEM((512, 2048), bf16),
             pltpu.VMEM((16, 2048), f32),
             pltpu.VMEM((16, 512), f32),
+            pltpu.VMEM((16, 512), f32),
             pltpu.VMEM((32, 512), f32),
             pltpu.VMEM((8, 512), f32),
+            pltpu.VMEM((512, 256), bf16),
+            pltpu.VMEM((256, 2048), bf16),
             pltpu.VMEM((80, 128), f32),
             pltpu.VMEM((3, 64, 128), f32),
             pltpu.VMEM((2, 8, 128), f32),
@@ -502,6 +532,34 @@
     )
 
 
+def put_out(forces, arrivals, forces_out, arrivals_out, sem):
+    copies = [
+        pltpu.make_async_copy(forces, forces_out, sem.at[0]),
+        pltpu.make_async_copy(arrivals, arrivals_out, sem.at[1]),
+    ]
+    for copy in copies:
+        copy.start()
+    for copy in copies:
+        copy.wait()
+
+
+def settle(forces, arrivals):
+    vmem = pl.BlockSpec(memory_space=pltpu.VMEM)
+    hbm = pl.BlockSpec(memory_space=pltpu.HBM)
+    return pl.pallas_call(
+        put_out,
+        out_shape=(
+            jax.ShapeDtypeStruct(forces.shape, f32),
+            jax.ShapeDtypeStruct(arrivals.shape, f32),
+        ),
+        in_specs=[vmem, vmem],
+        out_specs=(hbm, hbm),
+        scratch_shapes=[pltpu.SemaphoreType.DMA((2,))],
+        compiler_params=pltpu.CompilerParams(vmem_limit_bytes=8 << 20),
+        name="settle",
+    )(forces, arrivals)
+
+
 def solution(mesh):
     def cell(*dims):
         return P("gx", "gy", "gz", *[None] * len(dims))
@@ -509,7 +567,7 @@
     placed = (cell(0, 0), cell(0), cell(0), cell(0), cell(0), cell(0, 0), cell(0, 0), cell(0, 0))
     def step(positions, *rest):
         operands = [pltpu.with_memory_space_constraint(x, pltpu.HBM) for x in (jnp.swapaxes(positions, 2, 3), *rest)]
-        forces, arrivals = make_kernel(True)(*operands)
+        forces, arrivals = settle(*make_kernel(True)(*operands))
         return jnp.swapaxes(forces, 2, 3), arrivals
 
     return jax.shard_map(

time: 36.3 us -> 34 us (0.937)
  the two profiles are of different devices: /device:TPU:65 before, /device:TPU:9 now
where the time goes in v3:
time: 34 us; the launch traced here: 33.9 us
  Pallas kernels  33.2 us (98%)
  between operations  0.64 us (2%)
    pallas_call x1, Pallas kernels, step(): forces, arrivals = settle(*make_kernel(True)(*operands))  32.6 us

profile of v3, /device:TPU:9, one launch (start us, length us, event | category | flops | bytes accessed | tf_op | source)
XLA Modules:
  0.0 33.9 jit_solution(1249666648329581808)
XLA Ops:
  0.6 32.6 %force_step.1 = (f32[1,1,3,1,2048]{4,3,2,1,0:T(1,128)S(1)}, f32[1,1,1,2,8,128]{5,4,3,2,1,0:T(8,128)S(1)}) custom-call(f32[1,1,3,1,2048]{4,3,2,1,0:T(1,128)} %bitcast.4, f32[1,1,1,2048]{3,2,1,0:T(1,128)} %refs_1_.1, f32[1,1,1,2048]{3,2,1,0:T(1,128)} %refs_2_.1, f32[1,1,1,512]{3,2,1,0:T(1,128)} %refs_3_.1, s32[1,1,1,2048]{3,2,1,0:T(1,128)} %refs_4_.1, ...), custom_call_target="tpu_custom_call" | custom-call | tf_op jit(solution)/shard_map/force_step/pallas_call | solution.py:570
  33.3 0.6 %settle.1 = (f32[1,1,3,1,2048]{4,3,2,1,0:T(1,128)}, f32[1,1,1,2,8,128]{5,4,3,2,1,0:T(8,128)}) custom-call(f32[1,1,3,1,2048]{4,3,2,1,0:T(1,128)S(1)} %get-tuple-element.6.forces, f32[1,1,1,2,8,128]{5,4,3,2,1,0:T(8,128)S(1)} %get-tuple-element.7.arrivals), custom_call_target="tpu_custom_call" | custom-call | tf_op jit(solution)/shard_map/settle/pallas_call | solution.py:549

commit v4 on v3

--- a/solution.py
+++ b/solution.py
@@ -431,15 +431,12 @@
             copy.start()
     for s in POLES:
         build_cell(s, pay, bmat, rmat)
-    when(has_atomic, lambda: atomic_phase(POLES, False, *shared))
-    if comm:
-        for s in SIDES:
+    for n, s in enumerate(SIDES):
+        if comm:
             copies[s].wait_recv()
-        for copy in near_copies:
-            copy.start()
-    for s in SIDES:
+            near_copies[n].start()
         build_cell(s, pay, bmat, rmat)
-    when(has_atomic, lambda: atomic_phase(SIDES, False, *shared))
+    when(has_atomic, lambda: atomic_phase(POLES + SIDES, False, *shared))
     if comm:
         for copy in far_copies + near_arrivals:
             copy.wait_recv()

time: 34 us -> 33.9 us (level)
  the two profiles are of different devices: /device:TPU:9 before, /device:TPU:30 now
where the time goes in v4:
time: 33.9 us; the launch traced here: 33.8 us
  Pallas kernels  33.2 us (98%)
  between operations  0.64 us (2%)
    pallas_call x1, Pallas kernels, step(): forces, arrivals = settle(*make_kernel(True)(*operands))  32.5 us

profile of v4, /device:TPU:30, one launch (start us, length us, event | category | flops | bytes accessed | tf_op | source)
XLA Modules:
  0.0 33.8 jit_solution(5209927298922233236)
XLA Ops:
  0.6 32.5 %force_step.1 = (f32[1,1,3,1,2048]{4,3,2,1,0:T(1,128)S(1)}, f32[1,1,1,2,8,128]{5,4,3,2,1,0:T(8,128)S(1)}) custom-call(f32[1,1,3,1,2048]{4,3,2,1,0:T(1,128)} %bitcast.4, f32[1,1,1,2048]{3,2,1,0:T(1,128)} %refs_1_.1, f32[1,1,1,2048]{3,2,1,0:T(1,128)} %refs_2_.1, f32[1,1,1,512]{3,2,1,0:T(1,128)} %refs_3_.1, s32[1,1,1,2048]{3,2,1,0:T(1,128)} %refs_4_.1, ...), custom_call_target="tpu_custom_call" | custom-call | tf_op jit(solution)/shard_map/force_step/pallas_call | solution.py:567
  33.2 0.6 %settle.1 = (f32[1,1,3,1,2048]{4,3,2,1,0:T(1,128)}, f32[1,1,1,2,8,128]{5,4,3,2,1,0:T(8,128)}) custom-call(f32[1,1,3,1,2048]{4,3,2,1,0:T(1,128)S(1)} %get-tuple-element.6.forces, f32[1,1,1,2,8,128]{5,4,3,2,1,0:T(8,128)S(1)} %get-tuple-element.7.arrivals), custom_call_target="tpu_custom_call" | custom-call | tf_op jit(solution)/shard_map/settle/pallas_call | solution.py:546

commit v5 on v4

--- a/solution.py
+++ b/solution.py
@@ -242,9 +242,8 @@
         bead_tile(b, (dist0, dist1)[b % 2], (dist1, dist0)[b % 2], lists, amat, bmat, rmat, wcol, gather)
 
 
-def prologue(pos, charge, mass, weight, mapping, table, pay, wide16, bead16, light16, beads):
+def prologue(pos, charge, mass, weight, mapping, table, pay, wide16, bead16, folded, beads):
     label = mapping[0, 0, 0:1, :]
-
     label16 = label.astype(jnp.int16)
 
     def rows_of_table(k, _):
@@ -255,6 +254,23 @@
         return 0
 
     lax.fori_loop(0, 16, rows_of_table, 0)
+    for g in range(16):
+        h, mid, l = split3(weight[0, 0, 0:1, g * 32 : g * 32 + 32])
+        folded[g : g + 1, 0:32] = h
+        folded[16 + g : 17 + g, 0:32] = mid
+        folded[32 + g : 33 + g, 0:32] = l
+    member = lax.broadcasted_iota(i32, (32, 2048), 0) == (label & 31)
+    got = dot_nn(folded[:, 0:32].astype(bf16), jnp.where(member, 1.0, 0.0).astype(bf16))
+    got = got[0:16] + got[16:32] + got[32:48]
+    group = lax.broadcasted_iota(i32, (16, 2048), 0) == lax.shift_right_logical(label, 5)
+    atom_weight = jnp.sum(jnp.where(group, got, 0.0), axis=0, keepdims=True)
+    qw = charge[0, 0, 0:1, :] * atom_weight
+    for t in range(16):
+        cut = slice(t * 128, t * 128 + 128)
+        for k in range(3):
+            pay[OWN, 4 * t + k : 4 * t + k + 1, :] = pos[0, 0, k, 0:1, cut] - 0.5
+        pay[OWN, 4 * t + 3 : 4 * t + 4, :] = qw[:, cut]
+
     wide16[12:16, :] = jnp.zeros((4, 2048), f32)
     m = mass[0, 0, 0:1, :]
     for k in range(3):
@@ -271,18 +287,6 @@
     beads[0:3, :] = sums[0:3] / sums[3:4]
     beads[6:7, :] = weight[0, 0, 0:1, :]
     beads[7:8, :] = sums[3:4]
-    light16[...] = jnp.zeros((16, 512), f32)
-    h, mid, l = split3(weight[0, 0, 0:1, :])
-    light16[0:1, :] = h
-    light16[1:2, :] = mid
-    light16[2:3, :] = l
-    atom_weight = jnp.sum(dot_nn(light16[...].astype(bf16), table[...]), axis=0, keepdims=True)
-    qw = charge[0, 0, 0:1, :] * atom_weight
-    for t in range(16):
-        cut = slice(t * 128, t * 128 + 128)
-        for k in range(3):
-            pay[OWN, 4 * t + k : 4 * t + k + 1, :] = pos[0, 0, k, 0:1, cut] - 0.5
-        pay[OWN, 4 * t + 3 : 4 * t + 4, :] = qw[:, cut]
     for b in range(4):
         cut = slice(b * 128, b * 128 + 128)
         pay[OWN, 64 + 4 * b : 67 + 4 * b, :] = beads[0:3, cut] - 0.5
@@ -355,7 +359,7 @@
         given, refs = refs[0], refs[1:]
     (
         forces, arrivals, pos, charge, mass, weight, mapping, atom_lists, bead_lists, leaving,
-        pay, bmat, rmat, amat, wcol, dist0, dist1, done0, done1, total, gather, table, wide16, bead16, light16, bead32, beads, picks, leavers, flat, flat3,
+        pay, bmat, rmat, amat, wcol, dist0, dist1, done0, done1, total, gather, table, wide16, bead16, folded, bead32, beads, picks, leavers, flat, flat3,
         parcel, landed, load_sem, send_sem, recv_sem, pass_send, pass_recv,
     ) = refs
     staged = (pos, charge, mass, weight, mapping, atom_lists, bead_lists, leaving)
@@ -410,7 +414,7 @@
         has_atomic = has_coarse = True
     for n in range(8):
         loads[n].wait()
-    prologue(pos, charge, mass, weight, mapping, table, pay, wide16, bead16, light16, beads)
+    prologue(pos, charge, mass, weight, mapping, table, pay, wide16, bead16, folded, beads)
     if comm:
         pl.semaphore_wait(barrier, len(PARTNERS))
         for s in POLES + SIDES:
@@ -507,7 +511,7 @@
             pltpu.VMEM((512, 2048), bf16),
             pltpu.VMEM((16, 2048), f32),
             pltpu.VMEM((16, 512), f32),
-            pltpu.VMEM((16, 512), f32),
+            pltpu.VMEM((48, 128), f32),
             pltpu.VMEM((32, 512), f32),
             pltpu.VMEM((8, 512), f32),
             pltpu.VMEM((512, 256), bf16),

time: 33.9 us -> 34 us (level)
  no operation moved by 1% of the time
where the time goes in v5:
time: 34 us; the launch traced here: 33.8 us
  Pallas kernels  33.2 us (98%)
  between operations  0.64 us (2%)
    pallas_call x1, Pallas kernels, step(): forces, arrivals = settle(*make_kernel(True)(*operands))  32.5 us

profile of v5, /device:TPU:30, one launch (start us, length us, event | category | flops | bytes accessed | tf_op | source)
XLA Modules:
  0.0 33.8 jit_solution(4710715449225340439)
XLA Ops:
  0.6 32.5 %force_step.1 = (f32[1,1,3,1,2048]{4,3,2,1,0:T(1,128)S(1)}, f32[1,1,1,2,8,128]{5,4,3,2,1,0:T(8,128)S(1)}) custom-call(f32[1,1,3,1,2048]{4,3,2,1,0:T(1,128)} %bitcast.4, f32[1,1,1,2048]{3,2,1,0:T(1,128)} %refs_1_.1, f32[1,1,1,2048]{3,2,1,0:T(1,128)} %refs_2_.1, f32[1,1,1,512]{3,2,1,0:T(1,128)} %refs_3_.1, s32[1,1,1,2048]{3,2,1,0:T(1,128)} %refs_4_.1, ...), custom_call_target="tpu_custom_call" | custom-call | tf_op jit(solution)/shard_map/force_step/pallas_call | solution.py:571
  33.2 0.6 %settle.1 = (f32[1,1,3,1,2048]{4,3,2,1,0:T(1,128)}, f32[1,1,1,2,8,128]{5,4,3,2,1,0:T(8,128)}) custom-call(f32[1,1,3,1,2048]{4,3,2,1,0:T(1,128)S(1)} %get-tuple-element.6.forces, f32[1,1,1,2,8,128]{5,4,3,2,1,0:T(8,128)S(1)} %get-tuple-element.7.arrivals), custom_call_target="tpu_custom_call" | custom-call | tf_op jit(solution)/shard_map/settle/pallas_call | solution.py:550
